TPU v7x, 256 devices: a whole 4x4x8 slice. The times are simulated.
256 devices in a mesh: rec: 32 (over z, y), src: 8 (over x, core).
Axes of the slice: x: 4, y: 4, z: 8, core: 2. Of those that a mesh axis runs over, the one named last changes fastest.
Arguments:
- kernel: float32 [2, 2, 5120, 5120], P(None, None, 'rec', 'src'), may hold values from -0.0625 to 0.0625
- traces: float32 [8, 896, 2, 2, 256], P('src', 'rec')
- acq_lists: int32 [8, 896], P('src', 'rec'), may hold values from 0 to 639, as said below
- counts: int32 [8, 32], P('src', 'rec'), may hold values from 1 to 28, as said below
Outputs:
- solution: float32 [5120, 2, 2, 256], P(('src', 'rec'))
- next_left: float32 [5120, 2, 2, 256], P(('rec', 'src'))
Inputs may be any that keep to these rules, and one draw needn't show every extreme that they name: `acq_lists`: an id a * 20 + k names row k of area a. Within each list the first counts[s, r] slots of the blocks name every id exactly once; other slots hold ids to be ignored. No block names more than 1 ids of one area, and every block that names an area names exactly 1 of its ids. `counts`: used slots of a block; in every list some block uses all 28.
All inputs are finite; a program needn't handle non-finite values.
Results may differ from a plain program's by a relative error of at most 0.00026.
Values sent between devices are 32-bit elements; how exact they have to be, the bound alone decides.
A program may use at most 64 MiB of HBM per device.

v0:
```python
import jax
import jax.numpy as jnp
from jax import lax
from jax.sharding import PartitionSpec as P

NR = 5120
FREQS = 2
SOURCES = 256
ITERS = 2


def kernel_apply(kernel, vector):
    highest = lax.Precision.HIGHEST
    real_part = jnp.einsum("fmc,cfn->mfn", kernel[0], vector[:, 0], precision=highest) - jnp.einsum(
        "fmc,cfn->mfn", kernel[1], vector[:, 1], precision=highest
    )
    imag_part = jnp.einsum("fmc,cfn->mfn", kernel[0], vector[:, 1], precision=highest) + jnp.einsum(
        "fmc,cfn->mfn", kernel[1], vector[:, 0], precision=highest
    )
    return jnp.stack([real_part, imag_part], axis=1)


def kernel_adjoint(kernel, vector):
    highest = lax.Precision.HIGHEST
    real_part = jnp.einsum("fmc,mfn->cfn", kernel[0], vector[:, 0], precision=highest) + jnp.einsum(
        "fmc,mfn->cfn", kernel[1], vector[:, 1], precision=highest
    )
    imag_part = jnp.einsum("fmc,mfn->cfn", kernel[0], vector[:, 1], precision=highest) - jnp.einsum(
        "fmc,mfn->cfn", kernel[1], vector[:, 0], precision=highest
    )
    return jnp.stack([real_part, imag_part], axis=1)


def widen(values):
    return values[None, None, :, None]


def rms_norm(vector):
    local_sum = jnp.sum(vector * vector, axis=(0, 1, 3))
    global_sum = lax.psum(local_sum, ("rec", "src"))
    return jnp.sqrt(global_sum / (2.0 * NR * SOURCES))


def on_device(kernel, traces, acq_lists, counts):
    highest = lax.Precision.HIGHEST
    my_area = lax.axis_index("rec")
    row_count = kernel.shape[2] // lax.axis_size("src")
    slot_count = traces.shape[1]
    width = traces.shape[2] * traces.shape[3] * traces.shape[4]
    row_iota = jnp.arange(row_count, dtype=jnp.int32)
    piece_traces = lax.all_gather(traces, "rec", axis=1, tiled=True)
    piece_ids = lax.all_gather(acq_lists, "rec", axis=1, tiled=True)
    piece_counts = lax.all_gather(counts, "rec", axis=1, tiled=True)
    span_slots = piece_ids.shape[1]
    slot_iota = jnp.arange(span_slots, dtype=jnp.int32)
    block_iota = jnp.arange(piece_counts.shape[1], dtype=jnp.int32)
    in_block = (slot_iota // slot_count)[:, None] == block_iota[None, :]
    limits = jnp.sum(jnp.where(in_block, piece_counts[0][None, :], 0), axis=1)
    filled = slot_iota % slot_count < limits
    list_ids = piece_ids[0]
    wanted = filled & (list_ids // row_count == my_area)
    selector = ((list_ids % row_count)[None, :] == row_iota[:, None]) & wanted[None, :]
    observed = jnp.dot(
        selector.astype(jnp.float32), piece_traces.reshape(span_slots, width), precision=highest
    )
    observed = observed.reshape(row_count, 2, FREQS, SOURCES)

    def adjoint(vector):
        spread = lax.all_gather(vector, "src", axis=0, tiled=True)
        return lax.psum_scatter(
            kernel_adjoint(kernel, spread), "rec", scatter_dimension=0, tiled=True
        )

    beta_norm = rms_norm(observed)
    left_unit = observed / widen(beta_norm)
    right_vec = adjoint(left_unit)
    alpha_norm = rms_norm(right_vec)
    right_unit = right_vec / widen(alpha_norm)
    search = right_unit
    solution = jnp.zeros(right_unit.shape, jnp.float32)
    phibar = beta_norm
    rhobar = alpha_norm
    next_left = observed
    for iteration in range(ITERS):
        forward_spread = lax.all_gather(right_unit, "rec", axis=0, tiled=True)
        next_left = (
            lax.psum_scatter(
                kernel_apply(kernel, forward_spread), "src", scatter_dimension=0, tiled=True
            )
            - widen(alpha_norm) * left_unit
        )
        beta_norm = rms_norm(next_left)
        left_unit = next_left / widen(beta_norm)
        rho_value = jnp.sqrt(rhobar * rhobar + beta_norm * beta_norm)
        cosine = rhobar / rho_value
        sine_value = beta_norm / rho_value
        phi_value = cosine * phibar
        phibar = sine_value * phibar
        solution = solution + widen(phi_value / rho_value) * search
        if iteration + 1 < ITERS:
            right_vec = adjoint(left_unit) - widen(beta_norm) * right_unit
            alpha_norm = rms_norm(right_vec)
            right_unit = right_vec / widen(alpha_norm)
            theta_value = sine_value * alpha_norm
            rhobar = -cosine * alpha_norm
            search = right_unit - widen(theta_value / rho_value) * search
    return (solution, next_left)


def solution(mesh):
    placed = (
        P(None, None, "rec", "src"),
        P("src", "rec", None, None, None),
        P("src", "rec"),
        P("src", "rec"),
    )
    return jax.shard_map(
        on_device,
        mesh=mesh,
        in_specs=placed,
        out_specs=(P(("src", "rec"), None, None, None), P(("rec", "src"), None, None, None)),
        check_vma=False,
    )
```

profile of v0, /device:TPU:1, one launch (start us, length us, event | category | flops | bytes accessed | tf_op | source)
XLA Modules:
  0.0 1147.3 jit_solution(5020311262918664336)
XLA Ops:
  12.1 20.3 %all-reduce.6 = (s32[896]{0:T(1024)S(1)}, s32[32]{0:T(128)S(1)}) all-reduce(s32[896]{0:T(1024)S(1)} %bitcast_dynamic-update-slice_fusion.1, s32[32]{0:T(128)S(1)} %bitcast_dynamic-update-slice_fusion), channel_id=1, replica_groups=mesh['rec'=32,'src'=8] {'rec'}, use_global_device_ids=true, to_apply=%add | all-reduce | flops 928 | bytes 7424
  32.6 59.6 %all-gather.4.cloned.1.call-done = f32[1,896,2,2,256]{4,3,2,0,1:T(2,128)} async-done(((f32[1,28,2,2,256]{4,3,2,0,1:T(2,128)}), f32[1,896,2,2,256]{4,3,2,0,1:T(2,128)}) %all-gather.4.cloned.1.call-update) | async-done | bytes 3670032 | tf_op jit(solution)/shard_map/all_gather | solution.py:51
  92.1 6.6 copy.66
  98.8 3.9 multiply_reduce_fusion.3
  102.7 77.6 %psum.35 = f32[2]{0:T(128)S(1)} all-reduce(f32[2]{0:T(128)S(1)} %get-tuple-element.32), channel_id=1, replica_groups=mesh['rec'=32,'src'=8] {'rec','src'}, use_global_device_ids=true, to_apply=%region_2.3 | all-reduce | flops 2 | bytes 16 | tf_op jit(solution)/shard_map/psum | solution.py:40
  180.4 14.0 %all_gather.24 = f32[160,2,2,256]{3,2,1,0:T(2,128)S(1)} all-gather(f32[20,2,2,256]{3,2,1,0:T(2,128)S(1)} %copy.43), channel_id=1, replica_groups=mesh['rec'=32,'src'=8] {'src'}, dimensions={0}, use_global_device_ids=true | all-gather | bytes 737280 | tf_op jit(solution)/shard_map/all_gather | solution.py:69
  194.7 1.4 fusion.38
  196.1 1.4 fusion.40
  197.6 1.5 fusion.4
  199.1 1.5 fusion.5
  200.6 1.7 pad_maximum_fusion
  202.3 5.1 copy.46
  208.2 146.3 %all-reduce.12.cloned.1.call-done = f32[640,2,2,256]{3,2,1,0:T(2,128)} async-done(((f32[640,2,2,256]{3,2,1,0:T(2,128)}), f32[640,2,2,256]{3,2,1,0:T(2,128)}) %all-reduce.12.cloned.1.call-update) | async-done | bytes 2621456
  355.6 78.4 %psum.36 = f32[2]{0:T(128)S(1)} all-reduce(f32[2]{0:T(128)S(1)} %get-tuple-element.17), channel_id=1, replica_groups=mesh['rec'=32,'src'=8] {'rec','src'}, use_global_device_ids=true, to_apply=%region_5.6 | all-reduce | flops 2 | bytes 16 | tf_op jit(solution)/shard_map/psum | solution.py:40
  435.0 71.0 %all-gather.6.cloned.1.call-done = f32[640,2,2,256]{3,2,1,0:T(2,128)} async-done(((f32[20,2,2,256]{3,2,1,0:T(2,128)}), f32[640,2,2,256]{3,2,1,0:T(2,128)}) %all-gather.6.cloned.1.call-update) | async-done | bytes 2621456 | tf_op jit(solution)/shard_map/all_gather | solution.py:85
  506.0 2.6 fusion.73
  513.3 1.4 copy.51
  516.0 63.6 %all-reduce.14.cloned.1.call-done = f32[160,2,2,256]{3,2,1,0:T(2,128)} async-done(((f32[160,2,2,256]{3,2,1,0:T(2,128)}), f32[160,2,2,256]{3,2,1,0:T(2,128)}) %all-reduce.14.cloned.1.call-update) | async-done | bytes 655376
  580.7 78.5 %psum.37 = f32[2]{0:T(128)S(1)} all-reduce(f32[2]{0:T(128)S(1)} %multiply_reduce_fusion.2), channel_id=1, replica_groups=mesh['rec'=32,'src'=8] {'rec','src'}, use_global_device_ids=true, to_apply=%region_8.9 | all-reduce | flops 2 | bytes 16 | tf_op jit(solution)/shard_map/psum | solution.py:40
  659.4 14.2 %all_gather.26 = f32[160,2,2,256]{3,2,1,0:T(2,128)S(1)} all-gather(f32[20,2,2,256]{3,2,1,0:T(2,128)S(1)} %copy.53), channel_id=1, replica_groups=mesh['rec'=32,'src'=8] {'src'}, dimensions={0}, use_global_device_ids=true | all-gather | bytes 737280 | tf_op jit(solution)/shard_map/all_gather | solution.py:69
  673.8 1.4 fusion.32
  675.2 1.4 fusion.34
  676.7 1.5 fusion.2
  678.2 1.5 fusion.3
  679.7 1.7 pad_maximum_fusion.1
  681.4 5.1 copy.56
  686.6 147.7 %all-reduce.16.cloned.1.call-done = f32[640,2,2,256]{3,2,1,0:T(2,128)} async-done(((f32[640,2,2,256]{3,2,1,0:T(2,128)}), f32[640,2,2,256]{3,2,1,0:T(2,128)}) %all-reduce.16.cloned.1.call-update) | async-done | bytes 2621456
  835.4 78.4 %psum.38 = f32[2]{0:T(128)S(1)} all-reduce(f32[2]{0:T(128)S(1)} %multiply_reduce_fusion.1), channel_id=1, replica_groups=mesh['rec'=32,'src'=8] {'rec','src'}, use_global_device_ids=true, to_apply=%region_11.12 | all-reduce | flops 2 | bytes 16 | tf_op jit(solution)/shard_map/psum | solution.py:40
  914.9 70.9 %all-gather.8.cloned.1.call-done = f32[640,2,2,256]{3,2,1,0:T(2,128)} async-done(((f32[20,2,2,256]{3,2,1,0:T(2,128)}), f32[640,2,2,256]{3,2,1,0:T(2,128)}) %all-gather.8.cloned.1.call-update) | async-done | bytes 2621456 | tf_op jit(solution)/shard_map/all_gather | solution.py:85
  985.8 2.6 fusion.72
  994.5 64.9 %all-reduce.18.cloned.1.call-done = f32[160,2,2,256]{3,2,1,0:T(2,128)} async-done(((f32[160,2,2,256]{3,2,1,0:T(2,128)}), f32[160,2,2,256]{3,2,1,0:T(2,128)}) %all-reduce.18.cloned.1.call-update) | async-done | bytes 655376
  1060.5 78.5 %psum.39 = f32[2]{0:T(128)S(1)} all-reduce(f32[2]{0:T(128)S(1)} %get-tuple-element.15), channel_id=1, replica_groups=mesh['rec'=32,'src'=8] {'rec','src'}, use_global_device_ids=true, to_apply=%region_14.15 | all-reduce | flops 2 | bytes 16 | tf_op jit(solution)/shard_map/psum | solution.py:40
  (67 shorter events, 23.8 us)
Async XLA Ops:
  7.2 85.0 %all-gather.4.cloned.1.call-start = ((), (), s32[]{:S(2)}) async-start(), calls=%async_computation | async-start | bytes 3784704 | tf_op jit(solution)/shard_map/all_gather | solution.py:51
  7.9 346.6 %all-reduce.12.cloned.1.call-start = ((), (), s32[]{:S(2)}) async-start(), calls=%async_computation.3 | async-start | bytes 5242880
  102.7 92.0 %copy-start = (f32[2,2,160,640]{3,2,1,0:T(8,128)S(1)}, f32[2,2,160,640]{3,2,1,0:T(8,128)}, u32[]{:S(2)}) copy-start(f32[2,2,160,640]{3,2,1,0:T(8,128)} %param.4) | copy-start | bytes 4915204
  207.5 298.6 %all-gather.6.cloned.1.call-start = ((), (), s32[]{:S(2)}) async-start(), calls=%async_computation.1 | async-start | bytes 2703360 | tf_op jit(solution)/shard_map/all_gather | solution.py:85
  434.8 144.9 %all-reduce.14.cloned.1.call-start = ((), (), s32[]{:S(2)}) async-start(), calls=%async_computation.4 | async-start | bytes 1310720
  513.3 1.5 copy-start.1
  514.7 319.6 %all-reduce.16.cloned.1.call-start = ((), (), s32[]{:S(2)}) async-start(), calls=%async_computation.5 | async-start | bytes 5242880
  686.6 299.3 %all-gather.8.cloned.1.call-start = ((), (), s32[]{:S(2)}) async-start(), calls=%async_computation.2 | async-start | bytes 2703360 | tf_op jit(solution)/shard_map/all_gather | solution.py:85
  914.6 144.8 %all-reduce.18.cloned.1.call-start = ((), (), s32[]{:S(2)}) async-start(), calls=%async_computation.6 | async-start | bytes 1310720
Sparse Core Ops, SparseCore 0:
  10.6 81.5 all-gather.3
  207.6 146.8 all-reduce.11
  434.9 71.0 all-gather.5
  514.8 64.7 all-reduce.13
  686.7 147.5 all-reduce.15
  914.7 71.0 all-gather.7
  994.6 64.7 all-reduce.17
where the time goes:
time: 1150 us
  waiting for transfers between devices  625 us (54%)
  blocking collectives  440 us (38%)
  local copies, waits for them, and re-layouts  34.2 us (3%)
  matrix products  24.8 us (2%)
  between operations  17 us (1%)
    unnamed x11, waiting for transfers between devices  423 us
    psum x5, blocking collectives, rms_norm(): global_sum = lax.psum(local_sum, ('rec', 'src'))  391 us
    all_gather x2, waiting for transfers between devices, on_device(): forward_spread = lax.all_gather(right_unit, 'rec', axis=0, tiled=True)  142 us
    all_gather x1, waiting for transfers between devices, on_device(): piece_traces = lax.all_gather(traces, 'rec', axis=1, tiled=True)  59.6 us
    all_gather x2, blocking collectives, adjoint(): spread = lax.all_gather(vector, 'src', axis=0, tiled=True)  28.2 us
  transfers between devices with their start and end apart: 7, of which 7 were waited for; matrix products, arithmetic and copies ran while one was open for 0% of the time, Pallas kernels for 0%

commit v1 on v0

v1 whole, which is shorter than its diff:
```python
import functools
import jax
import jax.numpy as jnp
from jax import lax
from jax.experimental import pallas as pl
from jax.experimental.pallas import tpu as pltpu
from jax.sharding import PartitionSpec as P

NR = 5120
FREQS = 2
SOURCES = 256
ITERS = 2
NZ, NY, NX = 8, 4, 4
ROWS = 20
LANES = 512
BLK = 40
ROWS_REC = 160
COLS = 1280
MESH = pltpu.DeviceIdType.MESH if hasattr(pltpu, "DeviceIdType") else pl.DeviceIdType.MESH
F32 = jnp.float32
BF16 = jnp.bfloat16
COUNT = 2.0 * NR * SOURCES

ROWS_A = (0, 16)
ROWS_B = (16, 24)


class Copies:
    def __init__(self):
        self.names = {}

    def number(self, name):
        return self.names.setdefault(name, len(self.names))


def kernel_body(copies, k_hbm, traces, meta, sol_out, left_out, *scratch):
    (kf, s3, sp, kt3, p, vall, vh, vl, wst, uall, q, tbuf, mbuf, send_e, recv_e1, send_e2, recv_e2,
     rza, ryb, rzb, rya, rxq, nown, nx, ny, nz, left, vprev, wvec, sol, scal,
     ostage, orecv, ssem, rsem, lsem) = scratch
    r = lax.axis_index("rec")
    s = lax.axis_index("src")
    z, y = r // NY, r % NY
    x, c = s // 2, s % 2
    oc = 1 - c

    def dev(dz=0, dy=0, dx=0, flip=False):
        zz = lax.rem(z + dz + 2 * NZ, NZ)
        yy = lax.rem(y + dy + 2 * NY, NY)
        xx = lax.rem(x + dx + 2 * NX, NX)
        return (zz * NY + yy, xx * 2 + (oc if flip else c))

    def zat(d):
        return lax.rem(z + d + 2 * NZ, NZ)

    def yat(d):
        return lax.rem(y + d + 2 * NY, NY)

    def xat(d):
        return lax.rem(x + d + 2 * NX, NX)

    pending = []

    def send(name, src, dst, target):
        i = copies.number(name)
        copy = pltpu.make_async_remote_copy(
            src_ref=src, dst_ref=dst, send_sem=ssem.at[i], recv_sem=rsem.at[i],
            device_id=target, device_id_type=MESH)
        copy.start()
        pending.append(copy)

    def recv(name, dst):
        i = copies.number(name)
        pltpu.make_async_remote_copy(
            src_ref=dst, dst_ref=dst, send_sem=ssem.at[i], recv_sem=rsem.at[i],
            device_id=dev(flip=True), device_id_type=MESH).wait_recv()

    def flush():
        for copy in pending:
            copy.wait_send()
        pending.clear()

    own_k = pltpu.make_async_copy(k_hbm.at[:, c], kf.at[:, c], lsem.at[0])
    own_k.start()
    own_t = pltpu.make_async_copy(traces.at[c], tbuf.at[pl.ds(c * 32, 32)], lsem.at[1])
    own_t.start()
    barrier = pltpu.get_barrier_semaphore()
    friends = [dev(dz=d) for d in range(1, NZ)] + [dev(dy=d) for d in range(1, NY)]
    friends += [dev(dx=d) for d in range(1, NX)] + [dev(flip=True)]
    for friend in friends:
        pl.semaphore_signal(barrier, inc=1, device_id=friend, device_id_type=MESH)
    pl.semaphore_wait(barrier, len(friends))

    send("meta", meta, mbuf, dev(flip=True))
    send("traces", traces.at[oc], tbuf.at[pl.ds(c * 32, 32)], dev(flip=True))
    send("k", k_hbm.at[:, oc], kf.at[:, c], dev(flip=True))

    own_t.wait()
    recv("meta", mbuf)
    recv("traces", tbuf.at[pl.ds(oc * 32, 32)])
    ids = jnp.maximum(meta[0:1, :], mbuf[0:1, :])
    row = lax.broadcasted_iota(jnp.int32, (64, 128), 0)
    lane = lax.broadcasted_iota(jnp.int32, (64, 128), 1)
    area = (row >> 3) * NY + (row & 3)
    offset = ids - ROWS * area
    match = (offset >= 0) & (offset < ROWS) & ((lane >> 5) == ((row >> 2) & 1))
    picked = jnp.dot(jnp.where(match, 1.0, 0.0)[:, :64], tbuf[...],
                     preferred_element_type=F32, precision=lax.Precision.HIGHEST)
    place = jnp.sum(jnp.where(match, (offset + 1).astype(F32), 0.0), axis=1, keepdims=True)
    send_e[:, :, 0:LANES] = picked.reshape(NZ, 8, LANES)
    send_e[:, :, LANES:] = jnp.broadcast_to(place, (64, 128)).reshape(NZ, 8, 128)
    for d in (4, 3, 5, 2, 6, 1, 7):
        send(("e1", d), send_e.at[zat(d)], recv_e1.at[pl.ds(pl.multiple_of(z * 8, 8), 8)], dev(dz=d))
    recv_e1[pl.ds(pl.multiple_of(z * 8, 8), 8), :] = send_e[z]
    for d in (1, 7, 2, 6, 3, 5, 4):
        recv(("e1", d), recv_e1.at[pl.ds(pl.multiple_of(zat(-d) * 8, 8), 8)])
    swap = jnp.where(lane == (row & 15) * 4 + (row >> 4), 1.0, 0.0)[:, :64]
    send_e2[...] = jnp.dot(swap, recv_e1[...], preferred_element_type=F32,
                           precision=lax.Precision.HIGHEST).reshape(NY, 16, 640)
    for d in (2, 1, 3):
        send(("e2", d), send_e2.at[yat(d)], recv_e2.at[y], dev(dy=d))
    recv_e2[y] = send_e2[y]
    for d in (1, 3, 2):
        recv(("e2", d), recv_e2.at[yat(-d)])
    got = recv_e2[...].reshape(64, 640)
    slot = got[:, LANES:]
    wanted = slot - 1.0 + jnp.where((row & 1) == 1, float(ROWS), 0.0)
    onehot = jnp.where((slot > 0.5) & (lane.astype(F32) == wanted), 1.0, 0.0)
    left[...] = jnp.dot(jnp.transpose(onehot)[:BLK, :], got[:, :LANES],
                        preferred_element_type=F32, precision=lax.Precision.HIGHEST)

    own_k.wait()
    recv("k", kf.at[:, oc])
    for half in range(2):
        for part in range(2):
            cols = slice(half * 640, half * 640 + 640)
            value = kf[part, half]
            high = value.astype(BF16)
            low = (value - high.astype(F32)).astype(BF16)
            base = part * ROWS_REC
            s3[base:base + ROWS_REC, cols] = high
            s3[base + 320:base + 320 + ROWS_REC, cols] = low
            s3[base + 640:base + 640 + ROWS_REC, cols] = high

    def permute(i, carry):
        start = pl.multiple_of(i * 256, 256)
        new = lax.broadcasted_iota(jnp.int32, (256, COLS), 0) + start
        rec = (new * 1639) >> 16
        rest = new - rec * BLK
        second = rest >= ROWS
        old = jnp.where(second, 640 - ROWS, 0) + rec * ROWS + rest
        pick = jnp.where(lax.broadcasted_iota(jnp.int32, (256, COLS), 1) == old, 1.0, 0.0).astype(BF16)
        dims = (((1,), (1,)), ((), ()))
        sp[:, pl.ds(start, 256)] = lax.dot_general(
            s3[0:640, :], pick, dims, preferred_element_type=F32).astype(BF16)
        kt3[pl.ds(start, 256), :] = lax.dot_general(
            pick, s3[...], dims, preferred_element_type=F32).astype(BF16)
        return carry

    lax.fori_loop(0, COLS // 256, permute, 0)
    flush()

    def squares(value):
        squared = value * value
        total = squared[0:8, 0:128]
        for a in range(BLK // 8):
            for b in range(LANES // 128):
                if a or b:
                    total = total + squared[a * 8:a * 8 + 8, b * 128:b * 128 + 128]
        return total

    def norm_send(kind, axis, tile):
        size, buf, at, me = {"x": (NX, nx, xat, x), "y": (NY, ny, yat, y), "z": (NZ, nz, zat, z)}[axis]
        stage = {"x": 0, "y": 1, "z": 2}[axis]
        nown[kind, stage] = tile
        buf[kind, me] = tile
        for d in sorted(range(1, size), key=lambda d: -min(d, size - d)):
            send(("n", kind, axis, d), nown.at[kind, stage], buf.at[kind, me], dev(**{"d" + axis: d}))

    def norm_recv(kind, axis):
        size, buf, at = {"x": (NX, nx, xat), "y": (NY, ny, yat), "z": (NZ, nz, zat)}[axis]
        for d in range(1, size):
            recv(("n", kind, axis, d), buf.at[kind, at(-d)])
        total = buf[kind, 0]
        for i in range(1, size):
            total = total + buf[kind, i]
        return total

    def root(tile):
        return jnp.sqrt(jnp.sum(tile, axis=(0, 1), keepdims=True) / COUNT)

    HALF_A = {1: pl.ds(0, 8), -1: pl.ds(8, 8)}
    ALL_A = pl.ds(0, 16)
    ALL_B = pl.ds(16, 24)

    def half_b(parity, way):
        if (parity % 2 == 0) == (way == 1):
            return pl.ds(16, 16)
        return pl.ds(32, 8)

    def size_of(ds):
        return ds.size

    def gather_x():
        for way in (1, -1):
            send(("gx", way, 1), uall.at[x], uall.at[x], dev(dx=way))
        for way in (1, -1):
            recv(("gx", way, 1), uall.at[xat(-way)])
            rows = pl.ds(0, 16) if way == 1 else pl.ds(16, 24)
            send(("gx", way, 2), uall.at[xat(-way), rows], uall.at[xat(-way), rows], dev(dx=way))
        for way in (1, -1):
            rows = pl.ds(0, 16) if way == 1 else pl.ds(16, 24)
            recv(("gx", way, 2), uall.at[xat(-2), rows])

    def scatter_x():
        for way in (1, -1):
            rows = pl.ds(0, 16) if way == 1 else pl.ds(16, 24)
            send(("sx", way, 1), q.at[xat(2), rows], rxq.at[0 if way == 1 else 1, 0, rows], dev(dx=way))
        for way in (1, -1):
            i = 0 if way == 1 else 1
            rows = pl.ds(0, 16) if way == 1 else pl.ds(16, 24)
            recv(("sx", way, 1), rxq.at[i, 0, rows])
            q[xat(way), rows] += rxq[i, 0, rows]
            send(("sx", way, 2), q.at[xat(way)], rxq.at[i, 1], dev(dx=way))
        for way in (1, -1):
            recv(("sx", way, 2), rxq.at[0 if way == 1 else 1, 1])
        return q[x] + rxq[0, 1] + rxq[1, 1]

    WAYS = (1, -1)

    def wi(way):
        return 0 if way == 1 else 1

    def za_rows(way, t):
        return HALF_A[way] if t == 1 else ALL_A

    def za_send(way, t, g):
        rows = za_rows(way, t)
        block = p.at[zat(way * (5 - t)), pl.ds(2 * g, 2), rows]
        send(("za", way, t, g), block, rza.at[wi(way), t - 1, g, :, pl.ds(0, size_of(rows))], dev(dz=way))

    def za_recv(way, t, g):
        rows = za_rows(way, t)
        n = size_of(rows)
        recv(("za", way, t, g), rza.at[wi(way), t - 1, g, :, pl.ds(0, n)])
        p[zat(way * (4 - t)), pl.ds(2 * g, 2), rows] += rza[wi(way), t - 1, g, :, pl.ds(0, n)]

    def yb_rows(d, way, t):
        return half_b(d, way) if t == 1 else ALL_B

    def yb_send(d, way, t):
        rows = yb_rows(d, way, t)
        block = p.at[zat(d), yat(way * (3 - t)), rows]
        send(("yb", d, way, t), block, ryb.at[d, wi(way), t - 1, pl.ds(0, size_of(rows))], dev(dy=way))

    def yb_recv(d, way, t):
        rows = yb_rows(d, way, t)
        n = size_of(rows)
        recv(("yb", d, way, t), ryb.at[d, wi(way), t - 1, pl.ds(0, n)])
        p[zat(d), yat(way * (2 - t)), rows] += ryb[d, wi(way), t - 1, pl.ds(0, n)]

    def zb_rows(way, t):
        return half_b(0, way) if t == 1 else ALL_B

    def zb_send(way, t):
        rows = zb_rows(way, t)
        block = p.at[zat(way * (5 - t)), y, rows]
        send(("zb", way, t), block, rzb.at[wi(way), t - 1, pl.ds(0, size_of(rows))], dev(dz=way))

    def zb_recv(way, t):
        rows = zb_rows(way, t)
        n = size_of(rows)
        recv(("zb", way, t), rzb.at[wi(way), t - 1, pl.ds(0, n)])
        p[zat(way * (4 - t)), y, rows] += rzb[wi(way), t - 1, pl.ds(0, n)]

    def ya_send(way, t):
        rows = HALF_A[way] if t == 1 else ALL_A
        block = p.at[z, yat(way * (3 - t)), rows]
        send(("ya", way, t), block, rya.at[wi(way), t - 1, pl.ds(0, size_of(rows))], dev(dy=way))

    def ya_recv(way, t):
        rows = HALF_A[way] if t == 1 else ALL_A
        n = size_of(rows)
        recv(("ya", way, t), rya.at[wi(way), t - 1, pl.ds(0, n)])
        p[z, yat(way * (2 - t)), rows] += rya[wi(way), t - 1, pl.ds(0, n)]

    def scatter_rec(between_one, between_two):
        order = (4, 3, 5, 2, 6, 1, 7, 0)
        for g in range(2):
            for way in WAYS:
                za_send(way, 1, g)
        for d in order:
            for way in WAYS:
                yb_send(d, way, 1)

        def yb_mid(d):
            for way in WAYS:
                yb_recv(d, way, 1)
                yb_send(d, way, 2)

        def yb_end(d):
            for way in WAYS:
                yb_recv(d, way, 2)

        def za_step(t):
            for g in range(2):
                for way in WAYS:
                    za_recv(way, t, g)
                    if t < 4:
                        za_send(way, t + 1, g)

        def zb_step(t):
            for way in WAYS:
                zb_recv(way, t)
                if t < 4:
                    zb_send(way, t + 1)

        def ya_start():
            for way in WAYS:
                ya_send(way, 1)

        yb_mid(4)
        between_one()
        za_step(1)
        yb_mid(3)
        yb_mid(5)
        za_step(2)
        yb_end(4)
        for way in WAYS:
            zb_send(way, 1)
        yb_mid(2)
        yb_mid(6)
        between_two()
        za_step(3)
        yb_end(3)
        yb_end(5)
        zb_step(1)
        yb_mid(1)
        yb_mid(7)
        za_step(4)
        ya_start()
        yb_end(2)
        yb_end(6)
        zb_step(2)
        yb_mid(0)
        for way in WAYS:
            ya_recv(way, 1)
            ya_send(way, 2)
        yb_end(1)
        yb_end(7)
        zb_step(3)
        yb_end(0)
        for way in WAYS:
            ya_recv(way, 2)
        zb_step(4)
        return p[z, y]

    def gather_rec(between):
        def bz_rows(way, t):
            return half_b(0, way) if t == 4 else ALL_B

        def bz_send(way, t):
            rows = bz_rows(way, t)
            block = vall.at[zat(-way * (t - 1)), y, rows]
            send(("bz", way, t), block, block, dev(dz=way))

        def bz_recv(way, t):
            recv(("bz", way, t), vall.at[zat(-way * t), y, bz_rows(way, t)])

        def by_rows(d, way, t):
            return half_b(d, way) if t == 2 else ALL_B

        def by_send(d, way, t):
            block = vall.at[zat(d), yat(-way * (t - 1)), by_rows(d, way, t)]
            send(("by", d, way, t), block, block, dev(dy=way))

        def by_recv(d, way, t):
            recv(("by", d, way, t), vall.at[zat(d), yat(-way * t), by_rows(d, way, t)])

        def ay_send(way, t):
            block = vall.at[z, yat(-way * (t - 1)), HALF_A[way] if t == 2 else ALL_A]
            send(("ay", way, t), block, block, dev(dy=way))

        def ay_recv(way, t):
            recv(("ay", way, t), vall.at[z, yat(-way * t), HALF_A[way] if t == 2 else ALL_A])

        def az_rows(way, t):
            return HALF_A[way] if t == 4 else ALL_A

        def az_send(way, t, g):
            block = vall.at[zat(-way * (t - 1)), pl.ds(2 * g, 2), az_rows(way, t)]
            send(("az", way, t, g), block, block, dev(dz=way))

        def az_recv(way, t, g):
            recv(("az", way, t, g), vall.at[zat(-way * t), pl.ds(2 * g, 2), az_rows(way, t)])

        def by_start(d):
            for way in WAYS:
                by_send(d, way, 1)

        def by_mid(d):
            for way in WAYS:
                by_recv(d, way, 1)
                by_send(d, way, 2)

        def bz_step(t):
            for way in WAYS:
                bz_recv(way, t)
                if t < 4:
                    bz_send(way, t + 1)
            if t < 4:
                by_start(t)
                by_start(8 - t)
            else:
                by_start(4)

        def az_step(t):
            for g in range(2):
                for way in WAYS:
                    az_recv(way, t, g)
                    if t < 4:
                        az_send(way, t + 1, g)

        for way in WAYS:
            ay_send(way, 1)
            bz_send(way, 1)
        by_start(0)
        for way in WAYS:
            ay_recv(way, 1)
            ay_send(way, 2)
        bz_step(1)
        for way in WAYS:
            ay_recv(way, 2)
        for g in range(2):
            for way in WAYS:
                az_send(way, 1, g)
        by_mid(0)
        bz_step(2)
        between()
        by_mid(1)
        by_mid(7)
        az_step(1)
        bz_step(3)
        by_mid(2)
        by_mid(6)
        bz_step(4)
        az_step(2)
        by_mid(3)
        by_mid(5)
        az_step(3)
        by_mid(4)
        for d in (0, 1, 7, 2, 6, 3, 5, 4):
            for way in WAYS:
                by_recv(d, way, 2)
        az_step(4)

    def adjoint_products():
        value = uall[...].reshape(ROWS_REC, LANES)
        real, imag = value[:, :SOURCES], value[:, SOURCES:]
        for base, both in ((0, (real, imag)), (ROWS_REC, (imag, -real))):
            for i in range(2):
                cols = slice(i * SOURCES, i * SOURCES + SOURCES)
                high = both[i].astype(BF16)
                wst[base:base + ROWS_REC, cols] = high
                wst[base + 320:base + 320 + ROWS_REC, cols] = high
                wst[base + 640:base + 640 + ROWS_REC, cols] = (both[i] - high.astype(F32)).astype(BF16)

        def tile(i, carry):
            start = pl.multiple_of(i * 320, 320)
            out = jnp.dot(kt3[pl.ds(start, 320), :], wst[...], preferred_element_type=F32)
            p[pl.ds(i * 2, 2)] = out.reshape(2, NY, BLK, LANES)
            return carry

        lax.fori_loop(0, 4, tile, 0)

    def forward_products():
        def parts(i, carry):
            value = vall[i].reshape(NY * BLK, LANES)
            high = value.astype(BF16)
            rows = pl.ds(pl.multiple_of(i * 160, 160), 160)
            vh[rows, :] = high
            vl[rows, :] = (value - high.astype(F32)).astype(BF16)
            return carry

        lax.fori_loop(0, NZ, parts, 0)
        outs = []
        for i in range(2):
            cols = slice(i * SOURCES, i * SOURCES + SOURCES)
            one = jnp.dot(sp[...], vh[:, cols], preferred_element_type=F32)
            two = jnp.dot(sp[0:320, :], vl[:, cols], preferred_element_type=F32)
            outs.append(one[0:320] + one[320:640] + two)
        real = outs[0][:ROWS_REC] - outs[1][ROWS_REC:]
        imag = outs[1][:ROWS_REC] + outs[0][ROWS_REC:]
        q[:, :, :SOURCES] = real.reshape(NX, BLK, SOURCES)
        q[:, :, SOURCES:] = imag.reshape(NX, BLK, SOURCES)

    vprev[...] = jnp.zeros_like(vprev)
    wvec[...] = jnp.zeros_like(wvec)
    sol[...] = jnp.zeros_like(sol)
    scal[...] = jnp.ones_like(scal)

    def iteration(it, carry):
        first = it == 0
        left_now = left[...]
        uall[x] = left_now
        norm_send(0, "x", squares(left_now))
        gather_x()
        adjoint_products()
        norm_send(0, "y", norm_recv(0, "x"))
        box = {}

        def one():
            norm_send(0, "z", norm_recv(0, "y"))

        def two():
            box["beta"] = root(norm_recv(0, "z"))

        summed = scatter_rec(one, two)
        flush()
        beta = box["beta"]
        alpha_old = scal[0, 0:1, 0:1]
        phibar_old = scal[1, 0:1, 0:1]
        rhobar_old = scal[2, 0:1, 0:1]
        right = summed / beta - beta * vprev[...]
        vall[z, y] = right
        norm_send(1, "y", squares(right))

        def three():
            norm_send(1, "z", norm_recv(1, "y"))

        gather_rec(three)
        rho = jnp.sqrt(rhobar_old * rhobar_old + beta * beta)
        cosine = rhobar_old / rho
        sine = beta / rho
        phi = cosine * phibar_old
        wold = wvec[...]
        sol[...] += jnp.where(first, 0.0, phi / rho) * wold
        forward_products()
        norm_send(1, "x", norm_recv(1, "z"))
        product = scatter_x()
        alpha = root(norm_recv(1, "x"))
        vnew = vall[z, y] / alpha
        theta = sine * alpha
        wvec[...] = vnew - jnp.where(first, 0.0, theta / rho) * wold
        vprev[...] = vnew
        next_left = product / alpha - alpha * (left_now / beta)
        left[...] = next_left
        scal[0] = jnp.broadcast_to(alpha, (8, 128))
        scal[1] = jnp.broadcast_to(jnp.where(first, beta, sine * phibar_old), (8, 128))
        scal[2] = jnp.broadcast_to(jnp.where(first, alpha, -cosine * alpha), (8, 128))
        flush()
        return carry

    lax.fori_loop(0, ITERS, iteration, 0)

    last = left[...]
    norm_send(2, "x", squares(last))

    def stage(i, value):
        ostage[i, 0, 0:ROWS] = value[:ROWS]
        ostage[i, 1, 0:ROWS] = value[ROWS:]

    stage(0, last)
    send(("out", 0), ostage.at[0, oc], orecv.at[0], dev(flip=True))
    norm_send(2, "y", norm_recv(2, "x"))
    norm_send(2, "z", norm_recv(2, "y"))
    beta = root(norm_recv(2, "z"))
    phibar = scal[1, 0:1, 0:1]
    rhobar = scal[2, 0:1, 0:1]
    rho = jnp.sqrt(rhobar * rhobar + beta * beta)
    phi = (rhobar / rho) * phibar
    stage(1, sol[...] + (phi / rho) * wvec[...])
    send(("out", 1), ostage.at[1, oc], orecv.at[1], dev(flip=True))

    for i, out in ((0, left_out), (1, sol_out)):
        recv(("out", i), orecv.at[i])
        mine = ostage[i, c, 0:ROWS]
        other = orecv[i, 0:ROWS]
        slab0 = jnp.where(c == 0, mine, other)
        slab1 = jnp.where(c == 0, other, mine)
        out[:, 0:256] = slab0[:, :SOURCES]
        out[:, 256:512] = slab1[:, :SOURCES]
        out[:, 512:768] = slab0[:, SOURCES:]
        out[:, 768:1024] = slab1[:, SOURCES:]
    flush()


COPIES = 320


def on_device(kernel, traces, acq_lists, counts):
    core = lax.axis_index("src") % 2
    slots = traces.shape[1]
    by_slab = jnp.transpose(traces[0], (2, 0, 1, 3)).reshape(FREQS, slots, LANES)
    by_slab = jnp.pad(by_slab, ((0, 0), (0, 32 - slots), (0, 0)))
    lane = jnp.arange(128, dtype=jnp.int32)
    padded = jnp.pad(acq_lists[0], (0, 32 - slots))
    inside = lane - core * 32
    used = (inside >= 0) & (inside < counts[0, 0])
    meta = jnp.where(used, jnp.tile(padded, 4), -1)
    meta = jnp.broadcast_to(meta[None, :], (8, 128)).astype(jnp.int32)
    vmem = pltpu.VMEM
    scratch = [
        vmem((2, 2, ROWS_REC, 640), F32),
        vmem((960, COLS), BF16),
        vmem((640, COLS), BF16),
        vmem((COLS, 960), BF16),
        vmem((NZ, NY, BLK, LANES), F32),
        vmem((NZ, NY, BLK, LANES), F32),
        vmem((COLS, LANES), BF16),
        vmem((COLS, LANES), BF16),
        vmem((960, LANES), BF16),
        vmem((NX, BLK, LANES), F32),
        vmem((NX, BLK, LANES), F32),
        vmem((64, LANES), F32),
        vmem((8, 128), jnp.int32),
        vmem((NZ, 8, 640), F32),
        vmem((64, 640), F32),
        vmem((NY, 16, 640), F32),
        vmem((NY, 16, 640), F32),
        vmem((2, 4, 2, 2, 16, LANES), F32),
        vmem((8, 2, 2, 24, LANES), F32),
        vmem((2, 4, 24, LANES), F32),
        vmem((2, 2, 16, LANES), F32),
        vmem((2, 2, BLK, LANES), F32),
        vmem((3, 3, 8, 128), F32),
        vmem((3, NX, 8, 128), F32),
        vmem((3, NY, 8, 128), F32),
        vmem((3, NZ, 8, 128), F32),
        vmem((BLK, LANES), F32),
        vmem((BLK, LANES), F32),
        vmem((BLK, LANES), F32),
        vmem((BLK, LANES), F32),
        vmem((3, 8, 128), F32),
        vmem((2, 2, 24, LANES), F32),
        vmem((2, 24, LANES), F32),
        pltpu.SemaphoreType.DMA((COPIES,)),
        pltpu.SemaphoreType.DMA((COPIES,)),
        pltpu.SemaphoreType.DMA((2,)),
    ]
    whole = pl.BlockSpec(memory_space=pltpu.VMEM)
    outs = pl.pallas_call(
        functools.partial(kernel_body, Copies()),
        out_shape=(jax.ShapeDtypeStruct((ROWS, 1024), F32),) * 2,
        in_specs=[pl.BlockSpec(memory_space=pl.ANY), whole, whole],
        out_specs=(whole, whole),
        scratch_shapes=scratch,
        compiler_params=pltpu.CompilerParams(
            collective_id=0, has_side_effects=True, vmem_limit_bytes=60 * 1024 * 1024),
    )(kernel, by_slab, meta)
    return tuple(out.reshape(ROWS, 2, FREQS, SOURCES) for out in outs)


def solution(mesh):
    placed = (
        P(None, None, "rec", "src"),
        P("src", "rec", None, None, None),
        P("src", "rec"),
        P("src", "rec"),
    )
    return jax.shard_map(
        on_device,
        mesh=mesh,
        in_specs=placed,
        out_specs=(P(("src", "rec"), None, None, None), P(("rec", "src"), None, None, None)),
        check_vma=False,
    )
```

time: 1150 us -> 196 us (0.17)
  waiting for transfers between devices: 625 us -> 0 us
  blocking collectives: 440 us -> 0 us
  Pallas kernels: 0 us -> 188 us
  local copies, waits for them, and re-layouts: 34.2 us -> 6.13 us
  matrix products: 24.8 us -> 0 us
  between operations: 17 us -> 1.3 us
    unnamed x11 -> x0, waiting for transfers between devices: 423 us -> none
    psum x5 -> x0, blocking collectives: 391 us -> none  [rms_norm(): global_sum = lax.psum(local_sum, ('rec', 'src'))]
    all_gather x3 -> x0, waiting for transfers between devices: 202 us -> none  [the longest x2 142 us: on_device(): forward_spread = lax.all_gather(right_unit, 'rec', axis=0, tiled=True)]
    pallas_call x0 -> x1, Pallas kernels: none -> 188 us  [on_device(): pl.pallas_call(functools.partial(kernel_body, Copies()), out_shape=(jax.S...]
    all_gather x2 -> x0, blocking collectives: 28.2 us -> none  [adjoint(): spread = lax.all_gather(vector, 'src', axis=0, tiled=True)]
    dot_general x17 -> x0, matrix products: 24.8 us -> none  [the longest x1 3.9 us: on_device(): jnp.dot(selector.astype(jnp.float32), piece_traces.reshape(span_slots, wi...]
    unnamed x1 -> x0, blocking collectives: 20.3 us -> none
    another operation x4 -> x2, local copies, waits for them, and re-layouts: 13 us -> 0.09 us  [on_device(): meta = jnp.where(used, jnp.tile(padded, 4), -1)]
  transfers between devices with their start and end apart: 7 -> 0, of which waited for: 7 -> 0; matrix products, arithmetic and copies ran while one was open for 0% -> 0% of each run, Pallas kernels for 0% -> 0%
where the time goes in v1:
time: 196 us; the launch traced here: 195 us
  Pallas kernels  188 us (96%)
  local copies, waits for them, and re-layouts  6.13 us (3%)
    pallas_call x1, Pallas kernels, on_device(): pl.pallas_call(functools.partial(kernel_body, Copies()), out_shape=(jax.S...  188 us

profile of v1, /device:TPU:1, one launch (start us, length us, event | category | flops | bytes accessed | tf_op | source)
XLA Modules:
  0.0 195.4 jit_solution(13554224848214500293)
XLA Ops:
  1.3 0.7 pad.9
  2.0 0.1 tile.10
  2.0 0.6 broadcast_in_dim.11.meta
  2.6 0.9 copy.7
  3.6 0.7 pad.8.traces
  4.2 187.9 %shard_map.59 = (f32[20,1024]{1,0:T(8,128)}, f32[20,1024]{1,0:T(8,128)}) custom-call(f32[2,2,160,640]{3,2,1,0:T(8,128)} %k_hbm.1, f32[2,32,512]{2,1,0:T(8,128)} %pad.8.traces, s32[8,128]{1,0:T(8,128)} %broadcast_in_dim.11.meta), custom_call_target="tpu_custom_call" | custom-call | tf_op jit(solution)/shard_map/pallas_call | solution.py:641
  192.2 1.6 reshape.27
  193.8 1.6 reshape.28
  (2 shorter events, 0.0 us)

commit v2 on v0

v2 whole, which is shorter than its diff:
```python
import functools
import jax
import jax.numpy as jnp
from jax import lax
from jax.experimental import pallas as pl
from jax.experimental.pallas import tpu as pltpu
from jax.sharding import PartitionSpec as P

NR = 5120
FREQS = 2
SOURCES = 256
ITERS = 2
NZ, NY, NX = 8, 4, 4
SIZE = {"x": NX, "y": NY, "z": NZ}
ROWS = 20
HALVES = 2
WIDE = SOURCES // HALVES
LANES = 2 * WIDE
BLK = 40
ROWS_REC = 160
COLS = 1280
COPIES = 80
GROUPS = 16
AHEAD = 4
MESH = pl.DeviceIdType.MESH
F32 = jnp.float32
BF16 = jnp.bfloat16
COUNT = 2.0 * NR * SOURCES
EXACT = lax.Precision.HIGHEST
NEVER = 1e9

RATE = 51e3
RATE_CHIP = 600e3
DELAY = {("c", 0): 0.9, ("z", 1): 2.5, ("z", 2): 3.1, ("z", 3): 3.7, ("z", 4): 4.3}
DELAY.update({(a, d): 2.8 + 0.2 * d for a in "xy" for d in (1, 2)})
WAYS = (1, -1)


class Plan:
    def __init__(self):
        self.now = 0.0
        self.link = {}
        self.arrived = {}
        self.counted = {}
        self.expected = {}
        self.events = {}
        self.numbers = {}
        self.tasks = []
        self.log = []

    def number(self, name):
        return self.numbers.setdefault(name, len(self.numbers))

    def add(self, task, rank=0):
        self.tasks.append([rank, len(self.log), task, None])
        self.log.append(rank)
        self.step(self.tasks[-1])

    def sent(self, key, axis, d, size):
        hops = min(d % SIZE[axis], -d % SIZE[axis]) if axis != "c" else 0
        if axis == "c":
            paths, load = [axis], size / RATE_CHIP
        elif 2 * hops == SIZE[axis]:
            paths, load = [(axis, 1), (axis, -1)], size * hops / 2 / RATE
        else:
            paths, load = [(axis, 1 if d % SIZE[axis] == hops else -1)], size * hops / RATE
        start = max([self.now] + [self.link.get(path, 0.0) for path in paths])
        for path in paths:
            self.link[path] = start + load
        came = start + load + DELAY[axis, hops]
        self.arrived[key] = max(self.arrived.get(key, 0.0), came)
        self.counted[key] = self.counted.get(key, 0) + size

    def mark(self, name):
        self.events[name] = self.now

    def ready(self, need):
        if need is None:
            return 0.0
        if need[0] == "r":
            if self.counted.get(need[1], 0) < need[2]:
                return NEVER
            return self.arrived[need[1]]
        return max(self.events.get(name, NEVER) for name in need[1])

    def step(self, entry):
        try:
            entry[3] = next(entry[2])
        except StopIteration:
            self.tasks.remove(entry)

    def run(self):
        while self.tasks:
            times = [self.ready(entry[3]) for entry in self.tasks]
            first = min(times)
            if first >= NEVER:
                raise ValueError("stuck")
            self.now = max(self.now, first)
            able = [e for e, t in zip(self.tasks, times) if t <= self.now]
            best = min(able, key=lambda e: (e[0], self.ready(e[3]), e[1]))
            self.step(best)


def rows_a(way, part):
    return pl.ds(0 if way == 1 else 8, 8) if part else pl.ds(0, 16)


def rows_b(way, part):
    if not part:
        return pl.ds(16, 24)
    return pl.ds(16, 16) if way == 1 else pl.ds(32, 8)


def ii(way):
    return 0 if way == 1 else 1


def kernel_body(k_hbm, traces, ids_ref, counts_ref, sol_out, left_out, *scratch):
    (kf, s3, sp, kt3, pick, p, vall, vh, vl, wst, uall, q, acc, tbuf, tsend, meta, mbuf,
     send_e, recv_e1, send_e2, recv_e2, rza1, rza2, ryb, rzb1, rzb2, rya, rxq, dummy, nown, nx, ny, nz,
     left, ostage, orecv, ssem, rsem, lsem) = scratch
    plan = Plan()
    r = lax.axis_index("rec")
    s = lax.axis_index("src")
    z, y = r // NY, r % NY
    x, c = s // 2, s % 2
    oc = 1 - c
    me = {"x": x, "y": y, "z": z}

    def at(axis, d):
        return lax.rem(me[axis] + d + 2 * SIZE[axis], SIZE[axis])

    def dev(axis, d):
        zz = at("z", d) if axis == "z" else z
        yy = at("y", d) if axis == "y" else y
        xx = at("x", d) if axis == "x" else x
        return (zz * NY + yy, xx * 2 + (oc if axis == "c" else c))

    pending = {}
    groups = {}

    def size_of(ref):
        size = 4
        for n in ref.shape:
            size *= n
        return size

    def waiting(size, i, sems):
        rows = dummy.at[pl.ds(0, size // 512)]
        return pltpu.make_async_copy(rows, rows, sems.at[i])

    def send(it, name, src, dst, axis, d, group):
        i = plan.number(name)
        g = groups.setdefault(group, len(groups))
        pltpu.make_async_remote_copy(
            src_ref=src, dst_ref=dst, send_sem=ssem.at[g], recv_sem=rsem.at[i],
            device_id=dev(axis, d), device_id_type=MESH).start()
        pending[group] = pending.get(group, 0) + size_of(src)
        plan.sent((it, name), axis, d, size_of(src))

    def wait_recv(it, name, size):
        yield ("r", (it, name), size)
        waiting(size, plan.number(name), rsem).wait()

    def flush(*names):
        for group in names:
            size = pending.pop(group, 0)
            if size:
                waiting(size, groups[group], ssem).wait()

    def need(*names):
        return ("e", names)

    def spend(us):
        plan.now += us

    own_k = pltpu.make_async_copy(k_hbm.at[:, c], kf.at[:, c], lsem.at[0])
    own_k.start()
    barrier = pltpu.get_barrier_semaphore()
    friends = [(a, d) for a in ("z", "y", "x") for d in range(1, SIZE[a])] + [("c", 0)]
    for friend in friends:
        pl.semaphore_signal(barrier, inc=1, device_id=dev(*friend), device_id_type=MESH)

    slots = traces.shape[1]
    lane_row = lax.broadcasted_iota(jnp.int32, (1, slots), 1)
    listed = jnp.where(lane_row < counts_ref[...], ids_ref[...], -1)
    meta[...] = jnp.full((8, 128), -1, jnp.int32)

    @pl.when(c == 0)
    def _():
        meta[0:1, 0:slots] = listed

    @pl.when(c == 1)
    def _():
        meta[0:1, 32:32 + slots] = listed

    blank = jnp.zeros((32, HALVES * LANES), F32)
    tbuf[pl.ds(pl.multiple_of(c * 32, 32), 32), :] = blank
    tsend[...] = blank
    for half in range(HALVES):
        for part in range(2):
            cols = slice(half * LANES + part * WIDE, half * LANES + part * WIDE + WIDE)
            lanes = slice(half * WIDE, half * WIDE + WIDE)
            slab0 = traces[0, :, part, 0, lanes]
            slab1 = traces[0, :, part, 1, lanes]
            tsend[0:slots, cols] = jnp.where(c == 0, slab1, slab0)
            tbuf[pl.ds(pl.multiple_of(c * 32, 32), slots), cols] = jnp.where(c == 0, slab0, slab1)
    pl.semaphore_wait(barrier, len(friends))
    send(0, "meta", meta, mbuf, "c", 0, "in")
    send(0, "traces", tsend, tbuf.at[pl.ds(c * 32, 32)], "c", 0, "in")
    send(0, "k", k_hbm.at[:, oc], kf.at[:, c], "c", 0, "in")

    row = lax.broadcasted_iota(jnp.int32, (64, 128), 0)
    lane = lax.broadcasted_iota(jnp.int32, (64, 128), 1)
    wide = HALVES * LANES

    def observe():
        yield from wait_recv(0, "meta", 4096)
        yield from wait_recv(0, "traces", size_of(tsend))
        ids = jnp.maximum(meta[0:1, :], mbuf[0:1, :])
        area = (row >> 3) * NY + (row & 3)
        offset = ids - ROWS * area
        match = (offset >= 0) & (offset < ROWS) & ((lane >> 5) == ((row >> 2) & 1))
        picked = jnp.dot(jnp.where(match, 1.0, 0.0)[:, :64], tbuf[...],
                         preferred_element_type=F32, precision=EXACT)
        place = jnp.sum(jnp.where(match, (offset + 1).astype(F32), 0.0), axis=1, keepdims=True)
        send_e[:, :, 0:wide] = picked.reshape(NZ, 8, wide)
        send_e[:, :, wide:] = jnp.broadcast_to(place, (64, 128)).reshape(NZ, 8, 128)
        spend(0.8)
        mine = pl.ds(pl.multiple_of(z * 8, 8), 8)
        for d in (4, 3, 5, 2, 6, 1, 7):
            send(0, "e1", send_e.at[at("z", d)], recv_e1.at[mine], "z", d, "in")
        recv_e1[mine, :] = send_e[z]
        yield from wait_recv(0, "e1", 7 * size_of(send_e.at[0]))
        swap = jnp.where(lane == (row & 15) * 4 + (row >> 4), 1.0, 0.0)[:, :64]
        send_e2[...] = jnp.dot(swap, recv_e1[...], preferred_element_type=F32,
                               precision=EXACT).reshape(NY, 16, wide + 128)
        spend(0.8)
        for d in (2, 1, 3):
            send(0, "e2", send_e2.at[at("y", d)], recv_e2.at[y], "y", d, "in")
        recv_e2[y] = send_e2[y]
        yield from wait_recv(0, "e2", 3 * size_of(send_e2.at[0]))
        got = recv_e2[...].reshape(64, wide + 128)
        slot = got[:, wide:]
        wanted = slot - 1.0 + jnp.where((row & 1) == 1, float(ROWS), 0.0)
        onehot = jnp.where((slot > 0.5) & (lane.astype(F32) == wanted), 1.0, 0.0)
        value = jnp.dot(jnp.transpose(onehot)[:BLK, :], got[:, :wide],
                        preferred_element_type=F32, precision=EXACT)
        spend(0.8)
        for h in range(HALVES):
            left[h] = value[:, h * LANES:h * LANES + LANES]
            plan.mark(("left", 0, h))

    def split_half(half):
        for part in range(2):
            cols = pl.ds(pl.multiple_of(half * 640, 128), 640)
            value = kf[part, half]
            high = value.astype(BF16)
            low = (value - high.astype(F32)).astype(BF16)
            base = part * ROWS_REC
            s3[base:base + ROWS_REC, cols] = high
            s3[base + 320:base + 320 + ROWS_REC, cols] = low
            s3[base + 640:base + 640 + ROWS_REC, cols] = high

    dims = (((1,), (1,)), ((), ()))

    def order_kernel():
        def build(i, carry):
            start = pl.multiple_of(i * 256, 256)
            new = lax.broadcasted_iota(jnp.int32, (256, 128), 0) + start
            rec = (new * 1639) >> 16
            rest = new - rec * BLK
            old = jnp.where(rest >= ROWS, 640 - ROWS, 0) + rec * ROWS + rest
            lanes = lax.broadcasted_iota(jnp.int32, (256, 128), 1)
            for j in range(COLS // 128):
                pick[pl.ds(start, 256), j * 128:j * 128 + 128] = jnp.where(
                    lanes + j * 128 == old, 1.0, 0.0).astype(BF16)
            return carry

        lax.fori_loop(0, COLS // 256, build, 0)
        spend(1.5)
        own_k.wait()
        split_half(c)
        spend(0.4)
        yield from wait_recv(0, "k", size_of(kf.at[:, 0]))
        split_half(oc)
        spend(0.4)

        def turned(i, carry):
            start = pl.multiple_of(i * 256, 256)
            kt3[pl.ds(start, 256), :] = lax.dot_general(
                pick[pl.ds(start, 256), :], s3[...], dims, preferred_element_type=F32).astype(BF16)
            return carry

        lax.fori_loop(0, COLS // 256, turned, 0)
        spend(3.0)
        plan.mark("kt3")
        yield need(("left", 0, 0))

        def straight(i, carry):
            start = pl.multiple_of(i * 256, 256)
            sp[:, pl.ds(start, 256)] = lax.dot_general(
                s3[0:640, :], pick[pl.ds(start, 256), :], dims, preferred_element_type=F32).astype(BF16)
            return carry

        yield need(("gx", 0, HALVES - 1))
        lax.fori_loop(0, COLS // 256, straight, 0)
        spend(2.5)
        plan.mark("sp")

    def squares(value):
        squared = value * value
        total = squared[0:8, 0:128]
        for a in range(BLK // 8):
            for b in range(LANES // 128):
                if a or b:
                    total = total + squared[a * 8:a * 8 + 8, b * 128:b * 128 + 128]
        return total

    sums = {}

    def norm(kind, it, axes):
        yield need(*[("sum", kind, it, h) for h in range(HALVES)])
        total = sums[kind, it, 0]
        for h in range(1, HALVES):
            total = total + sums[kind, it, h]
        flush(("n", kind))
        for axis in axes:
            buf = {"x": nx, "y": ny, "z": nz}[axis]
            size = SIZE[axis]
            nown[kind, "xyz".index(axis)] = total
            buf[kind, me[axis]] = total
            for d in sorted(range(1, size), key=lambda d: -min(d, size - d)):
                send(it, ("n", kind, axis), nown.at[kind, "xyz".index(axis)], buf.at[kind, me[axis]],
                     axis, d, ("n", kind))
            yield from wait_recv(it, ("n", kind, axis), (size - 1) * 4096)
            total = buf[kind, 0]
            for i in range(1, size):
                total = total + buf[kind, i]
            spend(0.05)
        sums[kind, it] = jnp.sqrt(jnp.sum(total, axis=(0, 1), keepdims=True) / COUNT)
        spend(0.2)
        plan.mark(("norm", kind, it))

    def gather_x(it, h):
        yield need(("left", it, h))
        flush(("gx", h))
        value = left[h]
        uall[h, x] = value
        for d in (2, 1, 3):
            send(it, ("gx", h), uall.at[h, x], uall.at[h, x], "x", d, ("gx", h))
        sums[0, it, h] = squares(value)
        spend(0.15)
        plan.mark(("sum", 0, it, h))
        yield from wait_recv(it, ("gx", h), 3 * size_of(uall.at[h, 0]))
        plan.mark(("gx", it, h))
        yield need("kt3")
        flush(("gr", h), ("sx", h))
        value = uall[h].reshape(ROWS_REC, LANES)
        real, imag = value[:, :WIDE], value[:, WIDE:]
        for base, both in ((0, (real, imag)), (ROWS_REC, (imag, -real))):
            for i in range(2):
                cols = slice(i * WIDE, i * WIDE + WIDE)
                high = both[i].astype(BF16)
                wst[base:base + ROWS_REC, cols] = high
                wst[base + 320:base + 320 + ROWS_REC, cols] = high
                wst[base + 640:base + 640 + ROWS_REC, cols] = (both[i] - high.astype(F32)).astype(BF16)

        def tile(i, carry):
            start = pl.multiple_of(i * 320, 320)
            out = jnp.dot(kt3[pl.ds(start, 320), :], wst[...], preferred_element_type=F32)
            p[h, pl.ds(i * 2, 2)] = out.reshape(2, NY, BLK, LANES)
            return carry

        lax.fori_loop(0, 4, tile, 0)
        spend(1.2)
        plan.mark(("p", it, h))

    ORDER = (4, 3, 5, 2, 6, 1, 7, 0)
    A, B = pl.ds(0, 16), pl.ds(16, 24)

    def za(it, h):
        yield need(("p", it, h))
        for way in WAYS:
            part = rows_a(way, True)
            send(it, ("za", h, way), p.at[h, at("z", 3 * way), :, A], rza1.at[h, ii(way), :, pl.ds(0, 16)],
                 "z", way, ("sr", h))
            send(it, ("za", h, way), p.at[h, at("z", 4 * way), :, part], rza1.at[h, ii(way), :, pl.ds(16, 8)],
                 "z", 2 * way, ("sr", h))
        for way in WAYS:
            send(it, ("za", h), p.at[h, at("z", way), :, A], rza2.at[h, ii(way)], "z", way, ("sr", h))
        for way in WAYS:
            yield from wait_recv(it, ("za", h, way), size_of(rza1.at[h, 0]))
            p[h, at("z", 2 * way), :, A] += rza1[h, ii(way), :, 0:16]
            p[h, at("z", 2 * way), :, rows_a(way, True)] += rza1[h, ii(way), :, 16:24]
            spend(0.12)
            send(it, ("za", h), p.at[h, at("z", 2 * way), :, A], rza2.at[h, 2 + ii(way)], "z", 2 * way, ("sr", h))
        yield from wait_recv(it, ("za", h), size_of(rza2.at[h]))
        p[h, z, :, A] += rza2[h, 0] + rza2[h, 1] + rza2[h, 2] + rza2[h, 3]
        spend(0.15)
        for d in (2, 1, 3):
            send(it, ("ya", h), p.at[h, z, at("y", d), A], rya.at[h, d - 1], "y", d, ("sr", h))
        yield from wait_recv(it, ("ya", h), size_of(rya.at[h]))
        p[h, z, y, A] += rya[h, 0] + rya[h, 1] + rya[h, 2]
        spend(0.06)
        plan.mark(("za", it, h))

    def yb(it, h, d):
        k = ORDER.index(d)
        if k < AHEAD:
            yield need(("p", it, h))
        else:
            yield need(("yb", it, h, ORDER[k - AHEAD]))
        for e in (2, 1, 3):
            send(it, ("yb", h, d), p.at[h, at("z", d), at("y", e), B], ryb.at[h, d, e - 1], "y", e, ("sr", h))
        yield from wait_recv(it, ("yb", h, d), size_of(ryb.at[h, 0]))
        p[h, at("z", d), y, B] += ryb[h, d, 0] + ryb[h, d, 1] + ryb[h, d, 2]
        spend(0.08)
        plan.mark(("yb", it, h, d))

    def zb(it, h, way):
        part = rows_b(way, True)
        yield need(("yb", it, h, 4))
        send(it, ("zb", h, way), p.at[h, at("z", 4 * way), y, part], rzb1.at[h, ii(way), pl.ds(24, part.size)],
             "z", 2 * way, ("sr", h))
        yield need(("yb", it, h, 3 * way % NZ))
        send(it, ("zb", h, way), p.at[h, at("z", 3 * way), y, B], rzb1.at[h, ii(way), pl.ds(0, 24)],
             "z", way, ("sr", h))
        yield need(("yb", it, h, 2 * way % NZ))
        yield from wait_recv(it, ("zb", h, way), (24 + part.size) * 4 * LANES)
        p[h, at("z", 2 * way), y, B] += rzb1[h, ii(way), 0:24]
        p[h, at("z", 2 * way), y, part] += rzb1[h, ii(way), 24:24 + part.size]
        spend(0.06)
        send(it, ("zb", h), p.at[h, at("z", 2 * way), y, B], rzb2.at[h, 2 + ii(way)], "z", 2 * way, ("sr", h))
        plan.mark(("zb", it, h, way))

    def zb_end(it, h):
        for way in WAYS:
            yield need(("yb", it, h, way % NZ))
            send(it, ("zb", h), p.at[h, at("z", way), y, B], rzb2.at[h, ii(way)], "z", way, ("sr", h))
        yield need(("yb", it, h, 0), *[("zb", it, h, way) for way in WAYS])
        yield from wait_recv(it, ("zb", h), size_of(rzb2.at[h]))
        p[h, z, y, B] += rzb2[h, 0] + rzb2[h, 1] + rzb2[h, 2] + rzb2[h, 3]
        spend(0.08)
        plan.mark(("zb", it, h))

    state = {}

    def right(it, h):
        yield need(("norm", 0, it), ("za", it, h), ("zb", it, h))
        beta = sums[0, it]
        value = p[h, z, y] / beta
        if it:
            value = value - beta * state["v", h]
        vall[h, z, y] = value
        state["right", h] = value
        spend(0.1)
        plan.mark(("right", it, h))
        sums[1, it, h] = squares(value)
        spend(0.15)
        plan.mark(("sum", 1, it, h))

    def bz(it, h):
        yield need(("right", it, h))
        own = vall.at[h, z, y, B]
        for d in (2, -2, 1, -1):
            send(it, ("bz", h, -d % NZ), own, own, "z", d, ("gr", h))
        for way in WAYS:
            yield from wait_recv(it, ("bz", h, -2 * way % NZ), 24 * 4 * LANES)
            block = vall.at[h, at("z", -2 * way), y, rows_b(way, True)]
            send(it, ("bz", h, 4), block, block, "z", 2 * way, ("gr", h))
            block = vall.at[h, at("z", -2 * way), y, B]
            send(it, ("bz", h, -3 * way % NZ), block, block, "z", way, ("gr", h))
            plan.mark(("bz", it, h, -2 * way % NZ))

    def by(it, h, d):
        if d == 0:
            yield need(("right", it, h))
        elif d in (2, 6):
            yield need(("bz", it, h, d))
        else:
            yield from wait_recv(it, ("bz", h, d), 24 * 4 * LANES)
        block = vall.at[h, at("z", d), y, B]
        for e in (2, 1, 3):
            send(it, ("by", h), block, block, "y", e, ("gr", h))
        plan.mark(("by", it, h, d))

    def az(it, h):
        yield need(("right", it, h))
        own = vall.at[h, z, y, A]
        for d in (2, 1, 3):
            send(it, ("ay", h), own, own, "y", d, ("gr", h))
        yield from wait_recv(it, ("ay", h), 3 * 16 * 4 * LANES)
        own = vall.at[h, z, :, A]
        for d in (2, -2):
            send(it, ("az", h, d), own, own, "z", d, ("gr", h))
        for d in (1, -1):
            send(it, ("az", h), own, own, "z", d, ("gr", h))
        for way in WAYS:
            yield from wait_recv(it, ("az", h, 2 * way), 64 * 4 * LANES)
            block = vall.at[h, at("z", -2 * way), :, A]
            send(it, ("az", h), block, block, "z", way, ("gr", h))
            block = vall.at[h, at("z", -2 * way), :, rows_a(way, True)]
            send(it, ("az", h), block, block, "z", 2 * way, ("gr", h))
        yield from wait_recv(it, ("az", h), 5 * 64 * 4 * LANES)
        plan.mark(("az", it, h))

    def forward(it, h):
        yield need("sp", ("az", it, h), *[("by", it, h, d) for d in range(NZ)])
        yield from wait_recv(it, ("by", h), NZ * 3 * 24 * 4 * LANES)
        flush(("gx", h), ("sr", h))

        def parts(i, carry):
            value = vall[h, i].reshape(NY * BLK, LANES)
            high = value.astype(BF16)
            rows = pl.ds(pl.multiple_of(i * 160, 160), 160)
            vh[rows, :] = high
            vl[rows, :] = (value - high.astype(F32)).astype(BF16)
            return carry

        lax.fori_loop(0, NZ, parts, 0)

        def tile(i, carry):
            rows = pl.ds(pl.multiple_of(i * 320, 320), 320)
            acc[rows, :] = jnp.dot(sp[rows, :], vh[...], preferred_element_type=F32)
            return carry

        lax.fori_loop(0, 2, tile, 0)
        both = acc[0:320, :] + acc[320:640, :] + jnp.dot(sp[0:320, :], vl[...], preferred_element_type=F32)
        real = both[:ROWS_REC, :WIDE] - both[ROWS_REC:, WIDE:]
        imag = both[:ROWS_REC, WIDE:] + both[ROWS_REC:, :WIDE]
        q[h, :, :, :WIDE] = real.reshape(NX, BLK, WIDE)
        q[h, :, :, WIDE:] = imag.reshape(NX, BLK, WIDE)
        spend(1.4)
        for d in (2, 1, 3):
            send(it, ("sx", h), q.at[h, at("x", d)], rxq.at[h, d - 1], "x", d, ("sx", h))
        yield from wait_recv(it, ("sx", h), size_of(rxq.at[h]))
        product = q[h, x] + rxq[h, 0] + rxq[h, 1] + rxq[h, 2]
        yield need(("norm", 1, it))
        alpha, beta = sums[1, it], sums[0, it]
        value = product / alpha - alpha * (left[h] / beta)
        left[h] = value
        spend(0.15)
        plan.mark(("left", it + 1, h))
        vnew = state["right", h] / alpha
        if it == 0:
            state["w", h] = vnew
            state["sol", h] = jnp.zeros((BLK, LANES), F32)
        else:
            rho, cosine, sine, phibar = rotation(it - 1)
            state["sol", h] = state["sol", h] + (cosine * phibar / rho) * state["w", h]
            state["w", h] = vnew - (sine * alpha / rho) * state["w", h]
        state["v", h] = vnew
        spend(0.3)
        plan.mark(("state", it, h))

    known = {}

    def rotation(it):
        if it not in known:
            beta = sums[0, it + 1]
            if it == 0:
                rhobar, phibar = sums[1, 0], sums[0, 0]
            else:
                rho, cosine, sine, phibar = rotation(it - 1)
                rhobar, phibar = -cosine * sums[1, it], sine * phibar
            rho = jnp.sqrt(rhobar * rhobar + beta * beta)
            known[it] = (rho, rhobar / rho, beta / rho, phibar)
        return known[it]

    def output(i, h, out):
        if i == 0:
            yield need(("left", ITERS, h))
            value = left[h]
            sums[0, ITERS, h] = squares(value)
            plan.mark(("sum", 0, ITERS, h))
        else:
            yield need(("norm", 0, ITERS), ("state", ITERS - 1, h))
            rho, cosine, sine, phibar = rotation(ITERS - 1)
            value = state["sol", h] + (cosine * phibar / rho) * state["w", h]
        ostage[i, h, 0, 0:ROWS] = value[:ROWS]
        ostage[i, h, 1, 0:ROWS] = value[ROWS:]
        spend(0.2)
        send(0, ("out", i, h), ostage.at[i, h, oc], orecv.at[i, h], "c", 0, "out")
        yield from wait_recv(0, ("out", i, h), size_of(orecv.at[i, h]))
        mine = ostage[i, h, c, 0:ROWS]
        other = orecv[i, h, 0:ROWS]
        slab = (jnp.where(c == 0, mine, other), jnp.where(c == 0, other, mine))
        for f in range(FREQS):
            for part in range(2):
                out[:, part, f, h * WIDE:h * WIDE + WIDE] = slab[f][:, part * WIDE:part * WIDE + WIDE]
        spend(0.2)

    plan.add(observe(), 0)
    for it in range(ITERS):
        plan.add(norm(0, it, "xyz"), 0)
        plan.add(norm(1, it, "yzx"), 0)
        for h in range(HALVES):
            plan.add(gather_x(it, h), 1 + h)
            plan.add(za(it, h), 1 + h)
            plan.add(zb_end(it, h), 1 + h)
            plan.add(bz(it, h), 1 + h)
            plan.add(az(it, h), 1 + h)
            for way in WAYS:
                plan.add(zb(it, h, way), 1 + h)
            for d in ORDER:
                plan.add(yb(it, h, d), 1 + h)
            for d in (0, 1, 7, 2, 6, 3, 5, 4):
                plan.add(by(it, h, d), 1 + h)
            plan.add(right(it, h), 1 + h)
            plan.add(forward(it, h), 1 + h)
    plan.add(norm(0, ITERS, "xyz"), 0)
    for h in range(HALVES):
        plan.add(output(0, h, left_out), 3)
        plan.add(output(1, h, sol_out), 2)
    plan.add(order_kernel(), 5)
    plan.run()
    flush(*list(pending))
    TOTAL.append((plan.now, dict(plan.events), (len(plan.numbers), len(groups))))


TOTAL = []


def on_device(kernel, traces, acq_lists, counts):
    vmem = pltpu.VMEM
    two = HALVES
    scratch = [
        vmem((2, 2, ROWS_REC, 640), F32),
        vmem((960, COLS), BF16),
        vmem((640, COLS), BF16),
        vmem((COLS, 960), BF16),
        vmem((COLS, COLS), BF16),
        vmem((two, NZ, NY, BLK, LANES), F32),
        vmem((two, NZ, NY, BLK, LANES), F32),
        vmem((COLS, LANES), BF16),
        vmem((COLS, LANES), BF16),
        vmem((960, LANES), BF16),
        vmem((two, NX, BLK, LANES), F32),
        vmem((two, NX, BLK, LANES), F32),
        vmem((640, LANES), F32),
        vmem((64, two * LANES), F32),
        vmem((32, two * LANES), F32),
        vmem((8, 128), jnp.int32),
        vmem((8, 128), jnp.int32),
        vmem((NZ, 8, two * LANES + 128), F32),
        vmem((64, two * LANES + 128), F32),
        vmem((NY, 16, two * LANES + 128), F32),
        vmem((NY, 16, two * LANES + 128), F32),
        vmem((two, 2, NY, 24, LANES), F32),
        vmem((two, 4, NY, 16, LANES), F32),
        vmem((two, NZ, 3, 24, LANES), F32),
        vmem((two, 2, 40, LANES), F32),
        vmem((two, 4, 24, LANES), F32),
        vmem((two, 3, 16, LANES), F32),
        vmem((two, 3, BLK, LANES), F32),
        vmem((8192, 128), F32),
        vmem((2, 3, 8, 128), F32),
        vmem((2, NX, 8, 128), F32),
        vmem((2, NY, 8, 128), F32),
        vmem((2, NZ, 8, 128), F32),
        vmem((two, BLK, LANES), F32),
        vmem((2, two, 2, 24, LANES), F32),
        vmem((2, two, 24, LANES), F32),
        pltpu.SemaphoreType.DMA((GROUPS,)),
        pltpu.SemaphoreType.DMA((COPIES,)),
        pltpu.SemaphoreType.DMA((1,)),
    ]
    whole = pl.BlockSpec(memory_space=pltpu.VMEM)
    return pl.pallas_call(
        kernel_body,
        out_shape=(jax.ShapeDtypeStruct((ROWS, 2, FREQS, SOURCES), F32),) * 2,
        in_specs=[pl.BlockSpec(memory_space=pl.ANY), whole, whole, whole],
        out_specs=(whole, whole),
        scratch_shapes=scratch,
        compiler_params=pltpu.CompilerParams(
            collective_id=0, has_side_effects=True, vmem_limit_bytes=60 * 1024 * 1024),
    )(kernel, traces, acq_lists, counts)


def solution(mesh):
    placed = (
        P(None, None, "rec", "src"),
        P("src", "rec", None, None, None),
        P("src", "rec"),
        P("src", "rec"),
    )
    return jax.shard_map(
        on_device,
        mesh=mesh,
        in_specs=placed,
        out_specs=(P(("src", "rec"), None, None, None), P(("rec", "src"), None, None, None)),
        check_vma=False,
    )
```

time: 1150 us -> 145 us (0.13)
  waiting for transfers between devices: 625 us -> 0 us
  blocking collectives: 440 us -> 0 us
  Pallas kernels: 0 us -> 141 us
  local copies, waits for them, and re-layouts: 34.2 us -> 3.05 us
  matrix products: 24.8 us -> 0 us
  between operations: 17 us -> 1.29 us
    unnamed x11 -> x0, waiting for transfers between devices: 423 us -> none
    psum x5 -> x0, blocking collectives: 391 us -> none  [rms_norm(): global_sum = lax.psum(local_sum, ('rec', 'src'))]
    all_gather x3 -> x0, waiting for transfers between devices: 202 us -> none  [the longest x2 142 us: on_device(): forward_spread = lax.all_gather(right_unit, 'rec', axis=0, tiled=True)]
    pallas_call x0 -> x1, Pallas kernels: none -> 141 us  [on_device(): pl.pallas_call(kernel_body, out_shape=(jax.ShapeDtypeStruct((ROWS, 2, FRE...]
    all_gather x2 -> x0, blocking collectives: 28.2 us -> none  [adjoint(): spread = lax.all_gather(vector, 'src', axis=0, tiled=True)]
    dot_general x17 -> x0, matrix products: 24.8 us -> none  [the longest x1 3.9 us: on_device(): jnp.dot(selector.astype(jnp.float32), piece_traces.reshape(span_slots, wi...]
    unnamed x1 -> x0, blocking collectives: 20.3 us -> none
    another operation x4 -> x0, local copies, waits for them, and re-layouts: 13 us -> none  [the longest x2 10.3 us: kernel_adjoint(): return jnp.stack([real_part, imag_part], axis=1)]
  transfers between devices with their start and end apart: 7 -> 0, of which waited for: 7 -> 0; matrix products, arithmetic and copies ran while one was open for 0% -> 0% of each run, Pallas kernels for 0% -> 0%
where the time goes in v2:
time: 145 us
  Pallas kernels  141 us (97%)
  local copies, waits for them, and re-layouts  3.05 us (2%)
    pallas_call x1, Pallas kernels, on_device(): pl.pallas_call(kernel_body, out_shape=(jax.ShapeDtypeStruct((ROWS, 2, FRE...  141 us
    unnamed x2, local copies, waits for them, and re-layouts  3.05 us

profile of v2, /device:TPU:1, one launch (start us, length us, event | category | flops | bytes accessed | tf_op | source)
XLA Modules:
  0.0 145.2 jit_solution(775305769595421057)
XLA Ops:
  1.3 140.9 %shard_map.59 = (f32[20,2,2,256]{3,2,1,0:T(2,128)}, f32[20,2,2,256]{3,2,1,0:T(2,128)}) custom-call(f32[2,2,160,640]{3,2,1,0:T(8,128)} %k_hbm.1, f32[1,28,2,2,256]{4,3,2,1,0:T(2,128)} %traces.1, s32[1,28]{1,0:T(1,128)} %ids_ref.1, s32[1,1]{1,0:T(1,128)S(6)} %copy.8.counts_ref), custom_call_target="tpu_custom_call" | custom-call | tf_op jit(solution)/shard_map/pallas_call | solution.py:670
  142.2 1.5 %copy.9 = f32[20,2,2,256]{3,2,1,0:T(2,128)} copy(f32[20,2,2,256]{3,2,1,0:T(2,128)} %get-tuple-element.4) | data formatting | bytes 163840
  143.7 1.5 %copy.10 = f32[20,2,2,256]{3,2,1,0:T(2,128)} copy(f32[20,2,2,256]{3,2,1,0:T(2,128)} %get-tuple-element.5) | data formatting | bytes 163840

commit v3 on v2

--- a/solution.py
+++ b/solution.py
@@ -1,4 +1,4 @@
-import functools
+import random
 import jax
 import jax.numpy as jnp
 from jax import lax
@@ -11,7 +11,7 @@
 SOURCES = 256
 ITERS = 2
 NZ, NY, NX = 8, 4, 4
-SIZE = {"x": NX, "y": NY, "z": NZ}
+SIZE = {"x": NX, "y": NY, "z": NZ, "w": NX * NY}
 ROWS = 20
 HALVES = 2
 WIDE = SOURCES // HALVES
@@ -19,9 +19,15 @@
 BLK = 40
 ROWS_REC = 160
 COLS = 1280
-COPIES = 80
+COPIES = 71
 GROUPS = 16
 AHEAD = 4
+SEED = 0
+NOISE = (0,)
+ZA_RELAY = ()
+AZ_RELAY = ()
+YB_RELAY = ()
+BY_RELAY = ()
 MESH = pl.DeviceIdType.MESH
 F32 = jnp.float32
 BF16 = jnp.bfloat16
@@ -39,6 +45,7 @@
 class Plan:
     def __init__(self):
         self.now = 0.0
+        self.noise = random.Random(SEED)
         self.link = {}
         self.arrived = {}
         self.counted = {}
@@ -52,12 +59,19 @@
         return self.numbers.setdefault(name, len(self.numbers))
 
     def add(self, task, rank=0):
+        rank += self.noise.choice(NOISE)
         self.tasks.append([rank, len(self.log), task, None])
         self.log.append(rank)
         self.step(self.tasks[-1])
 
     def sent(self, key, axis, d, size):
         hops = min(d % SIZE[axis], -d % SIZE[axis]) if axis != "c" else 0
+        if axis == "w":
+            dx, dy = d % NX, d // NX
+            far = min(dx, NX - dx) + min(dy, NY - dy)
+            self.arrived[key] = max(self.arrived.get(key, 0.0), self.now + 2.3 + 0.6 * far)
+            self.counted[key] = self.counted.get(key, 0) + size
+            return
         if axis == "c":
             paths, load = [axis], size / RATE_CHIP
         elif 2 * hops == SIZE[axis]:
@@ -115,9 +129,9 @@
     return 0 if way == 1 else 1
 
 
-def kernel_body(k_hbm, traces, ids_ref, counts_ref, sol_out, left_out, *scratch):
-    (kf, s3, sp, kt3, pick, p, vall, vh, vl, wst, uall, q, acc, tbuf, tsend, meta, mbuf,
-     send_e, recv_e1, send_e2, recv_e2, rza1, rza2, ryb, rzb1, rzb2, rya, rxq, dummy, nown, nx, ny, nz,
+def kernel_body(k_hbm, traces_hbm, ids_ref, counts_ref, sol_out, left_out, *scratch):
+    (traces, kf, s3, sp, kt3, pick, p, vall, vh, vl, wst, uall, q, acc, tbuf, tsend, meta, mbuf,
+     send_e, recv_e1, send_e2, recv_e2, rza1, rza2, ryb, rzb1, rzb2, rya, rxq, dummy, tiny, nown, nx, nz,
      left, ostage, orecv, ssem, rsem, lsem) = scratch
     plan = Plan()
     r = lax.axis_index("rec")
@@ -132,8 +146,8 @@
 
     def dev(axis, d):
         zz = at("z", d) if axis == "z" else z
-        yy = at("y", d) if axis == "y" else y
-        xx = at("x", d) if axis == "x" else x
+        yy = at("y", d // NX if axis == "w" else d) if axis in "yw" else y
+        xx = at("x", d % NX if axis == "w" else d) if axis in "xw" else x
         return (zz * NY + yy, xx * 2 + (oc if axis == "c" else c))
 
     pending = {}
@@ -146,7 +160,7 @@
         return size
 
     def waiting(size, i, sems):
-        rows = dummy.at[pl.ds(0, size // 512)]
+        rows = (dummy if size % 4096 == 0 else tiny).at[pl.ds(0, size // 512)]
         return pltpu.make_async_copy(rows, rows, sems.at[i])
 
     def send(it, name, src, dst, axis, d, group):
@@ -176,12 +190,14 @@
 
     own_k = pltpu.make_async_copy(k_hbm.at[:, c], kf.at[:, c], lsem.at[0])
     own_k.start()
+    own_t = pltpu.make_async_copy(traces_hbm, traces, lsem.at[1])
+    own_t.start()
     barrier = pltpu.get_barrier_semaphore()
-    friends = [(a, d) for a in ("z", "y", "x") for d in range(1, SIZE[a])] + [("c", 0)]
+    friends = [(a, d) for a in ("z", "w") for d in range(1, SIZE[a])] + [("c", 0)]
     for friend in friends:
         pl.semaphore_signal(barrier, inc=1, device_id=dev(*friend), device_id_type=MESH)
 
-    slots = traces.shape[1]
+    slots = traces_hbm.shape[1]
     lane_row = lax.broadcasted_iota(jnp.int32, (1, slots), 1)
     listed = jnp.where(lane_row < counts_ref[...], ids_ref[...], -1)
     meta[...] = jnp.full((8, 128), -1, jnp.int32)
@@ -197,6 +213,7 @@
     blank = jnp.zeros((32, HALVES * LANES), F32)
     tbuf[pl.ds(pl.multiple_of(c * 32, 32), 32), :] = blank
     tsend[...] = blank
+    own_t.wait()
     for half in range(HALVES):
         for part in range(2):
             cols = slice(half * LANES + part * WIDE, half * LANES + part * WIDE + WIDE)
@@ -324,20 +341,22 @@
         total = sums[kind, it, 0]
         for h in range(1, HALVES):
             total = total + sums[kind, it, h]
+        total = jnp.sum(total, axis=0, keepdims=True)
         flush(("n", kind))
         for axis in axes:
-            buf = {"x": nx, "y": ny, "z": nz}[axis]
+            buf = {"w": nx, "z": nz}[axis]
             size = SIZE[axis]
-            nown[kind, "xyz".index(axis)] = total
-            buf[kind, me[axis]] = total
-            for d in sorted(range(1, size), key=lambda d: -min(d, size - d)):
-                send(it, ("n", kind, axis), nown.at[kind, "xyz".index(axis)], buf.at[kind, me[axis]],
+            mine = z if axis == "z" else y * NX + x
+            nown[kind, "wz".index(axis)] = total
+            buf[kind, mine] = total
+            for d in range(1, size):
+                send(it, ("n", kind, axis), nown.at[kind, "wz".index(axis)], buf.at[kind, mine],
                      axis, d, ("n", kind))
-            yield from wait_recv(it, ("n", kind, axis), (size - 1) * 4096)
+            yield from wait_recv(it, ("n", kind, axis), (size - 1) * 512)
             total = buf[kind, 0]
             for i in range(1, size):
                 total = total + buf[kind, i]
-            spend(0.05)
+            spend(0.1)
         sums[kind, it] = jnp.sqrt(jnp.sum(total, axis=(0, 1), keepdims=True) / COUNT)
         spend(0.2)
         plan.mark(("norm", kind, it))
@@ -381,22 +400,25 @@
 
     def za(it, h):
         yield need(("p", it, h))
-        for way in WAYS:
-            part = rows_a(way, True)
-            send(it, ("za", h, way), p.at[h, at("z", 3 * way), :, A], rza1.at[h, ii(way), :, pl.ds(0, 16)],
-                 "z", way, ("sr", h))
-            send(it, ("za", h, way), p.at[h, at("z", 4 * way), :, part], rza1.at[h, ii(way), :, pl.ds(16, 8)],
-                 "z", 2 * way, ("sr", h))
-        for way in WAYS:
-            send(it, ("za", h), p.at[h, at("z", way), :, A], rza2.at[h, ii(way)], "z", way, ("sr", h))
-        for way in WAYS:
-            yield from wait_recv(it, ("za", h, way), size_of(rza1.at[h, 0]))
-            p[h, at("z", 2 * way), :, A] += rza1[h, ii(way), :, 0:16]
-            p[h, at("z", 2 * way), :, rows_a(way, True)] += rza1[h, ii(way), :, 16:24]
-            spend(0.12)
-            send(it, ("za", h), p.at[h, at("z", 2 * way), :, A], rza2.at[h, 2 + ii(way)], "z", 2 * way, ("sr", h))
-        yield from wait_recv(it, ("za", h), size_of(rza2.at[h]))
-        p[h, z, :, A] += rza2[h, 0] + rza2[h, 1] + rza2[h, 2] + rza2[h, 3]
+        if h in ZA_RELAY:
+            yield need(*[("zr", it, h, g) for g in range(2)])
+        else:
+            for way in WAYS:
+                part = rows_a(way, True)
+                send(it, ("za", h, way), p.at[h, at("z", 3 * way), :, A], rza1.at[h, ii(way), :, pl.ds(0, 16)],
+                     "z", way, ("sr", h))
+                send(it, ("za", h, way), p.at[h, at("z", 4 * way), :, part], rza1.at[h, ii(way), :, pl.ds(16, 8)],
+                     "z", 2 * way, ("sr", h))
+            for way in WAYS:
+                send(it, ("za", h), p.at[h, at("z", way), :, A], rza2.at[h, ii(way)], "z", way, ("sr", h))
+            for way in WAYS:
+                yield from wait_recv(it, ("za", h, way), size_of(rza1.at[h, 0]))
+                p[h, at("z", 2 * way), :, A] += rza1[h, ii(way), :, 0:16]
+                p[h, at("z", 2 * way), :, rows_a(way, True)] += rza1[h, ii(way), :, 16:24]
+                spend(0.12)
+                send(it, ("za", h), p.at[h, at("z", 2 * way), :, A], rza2.at[h, 2 + ii(way)], "z", 2 * way, ("sr", h))
+            yield from wait_recv(it, ("za", h), size_of(rza2.at[h]))
+            p[h, z, :, A] += rza2[h, 0] + rza2[h, 1] + rza2[h, 2] + rza2[h, 3]
         spend(0.15)
         for d in (2, 1, 3):
             send(it, ("ya", h), p.at[h, z, at("y", d), A], rya.at[h, d - 1], "y", d, ("sr", h))
@@ -405,16 +427,58 @@
         spend(0.06)
         plan.mark(("za", it, h))
 
+    def zr(it, h, g):
+        yield need(("p", it, h))
+        pair = pl.ds(2 * g, 2)
+        for way in WAYS:
+            part = rows_a(way, True)
+            send(it, ("zr", h, g, way, 1), p.at[h, at("z", 4 * way), pair, part],
+                 rza1.at[h, ii(way), pair, pl.ds(16, 8)], "z", way, ("sr", h))
+        for step in (1, 2, 3):
+            for way in WAYS:
+                part = rows_a(way, True)
+                yield from wait_recv(it, ("zr", h, g, way, step), (16 if step == 1 else 32) * 4 * LANES)
+                d = at("z", (4 - step) * way)
+                if step == 1:
+                    p[h, d, pair, part] += rza1[h, ii(way), pair, 16:24]
+                elif step == 2:
+                    p[h, d, pair, A] += rza1[h, ii(way), pair, 0:16]
+                else:
+                    p[h, d, pair, A] += rza2[h, 2 + ii(way), pair]
+                spend(0.06)
+                into = (None, rza1.at[h, ii(way), pair, pl.ds(0, 16)], rza2.at[h, 2 + ii(way), pair],
+                        rza2.at[h, ii(way), pair])[step]
+                name = ("zr", h, g, way, step + 1) if step < 3 else ("zr", h, g)
+                send(it, name, p.at[h, d, pair, A], into, "z", way, ("sr", h))
+        yield from wait_recv(it, ("zr", h, g), 2 * 32 * 4 * LANES)
+        p[h, z, pair, A] += rza2[h, 0, pair] + rza2[h, 1, pair]
+        spend(0.08)
+        plan.mark(("zr", it, h, g))
+
     def yb(it, h, d):
         k = ORDER.index(d)
         if k < AHEAD:
             yield need(("p", it, h))
         else:
             yield need(("yb", it, h, ORDER[k - AHEAD]))
-        for e in (2, 1, 3):
-            send(it, ("yb", h, d), p.at[h, at("z", d), at("y", e), B], ryb.at[h, d, e - 1], "y", e, ("sr", h))
-        yield from wait_recv(it, ("yb", h, d), size_of(ryb.at[h, 0]))
-        p[h, at("z", d), y, B] += ryb[h, d, 0] + ryb[h, d, 1] + ryb[h, d, 2]
+        if d in YB_RELAY:
+            for way in WAYS:
+                part = rows_b(way if d % 2 else -way, True)
+                send(it, ("yb", h, d, way), p.at[h, at("z", d), at("y", 2), part],
+                     ryb.at[h, d, 2, pl.ds(part.start - 16, part.size)], "y", way, ("sr", h))
+            for way in WAYS:
+                part = rows_b(way if d % 2 else -way, True)
+                yield from wait_recv(it, ("yb", h, d, way), part.size * 4 * LANES)
+                p[h, at("z", d), at("y", way), part] += ryb[h, d, 2, part.start - 16:part.start - 16 + part.size]
+                spend(0.05)
+                send(it, ("yb", h, d), p.at[h, at("z", d), at("y", way), B], ryb.at[h, d, ii(way)], "y", way, ("sr", h))
+            yield from wait_recv(it, ("yb", h, d), 2 * 24 * 4 * LANES)
+            p[h, at("z", d), y, B] += ryb[h, d, 0] + ryb[h, d, 1]
+        else:
+            for e in (2, 1, 3):
+                send(it, ("yb", h, d), p.at[h, at("z", d), at("y", e), B], ryb.at[h, d, e - 1], "y", e, ("sr", h))
+            yield from wait_recv(it, ("yb", h, d), size_of(ryb.at[h, 0]))
+            p[h, at("z", d), y, B] += ryb[h, d, 0] + ryb[h, d, 1] + ryb[h, d, 2]
         spend(0.08)
         plan.mark(("yb", it, h, d))
 
@@ -481,9 +545,33 @@
         else:
             yield from wait_recv(it, ("bz", h, d), 24 * 4 * LANES)
         block = vall.at[h, at("z", d), y, B]
-        for e in (2, 1, 3):
-            send(it, ("by", h), block, block, "y", e, ("gr", h))
+        if d in BY_RELAY:
+            for way in WAYS:
+                send(it, ("by", h, d, way), block, block, "y", way, ("gr", h))
+            plan.mark(("by", it, h, d))
+            for way in WAYS:
+                yield from wait_recv(it, ("by", h, d, way), 24 * 4 * LANES)
+                block = vall.at[h, at("z", d), at("y", -way), rows_b(way if d % 2 else -way, True)]
+                send(it, ("by", h), block, block, "y", way, ("gr", h))
+        else:
+            for e in (2, 1, 3):
+                send(it, ("by", h), block, block, "y", e, ("gr", h))
         plan.mark(("by", it, h, d))
+
+    def ar(it, h, g):
+        yield need(("ay", it, h))
+        pair = pl.ds(2 * g, 2)
+        own = vall.at[h, z, pair, A]
+        for way in WAYS:
+            send(it, ("ar", h, g, way, 1), own, own, "z", way, ("gr", h))
+        for step in (1, 2, 3):
+            for way in WAYS:
+                yield from wait_recv(it, ("ar", h, g, way, step), 32 * 4 * LANES)
+                rows = A if step < 3 else rows_a(way, True)
+                block = vall.at[h, at("z", -way * step), pair, rows]
+                send(it, ("ar", h, g, way, step + 1) if step < 3 else ("ar", h, g), block, block, "z", way, ("gr", h))
+        yield from wait_recv(it, ("ar", h, g), 32 * 4 * LANES)
+        plan.mark(("ar", it, h, g))
 
     def az(it, h):
         yield need(("right", it, h))
@@ -491,6 +579,11 @@
         for d in (2, 1, 3):
             send(it, ("ay", h), own, own, "y", d, ("gr", h))
         yield from wait_recv(it, ("ay", h), 3 * 16 * 4 * LANES)
+        plan.mark(("ay", it, h))
+        if h in AZ_RELAY:
+            yield need(*[("ar", it, h, g) for g in range(2)])
+            plan.mark(("az", it, h))
+            return
         own = vall.at[h, z, :, A]
         for d in (2, -2):
             send(it, ("az", h, d), own, own, "z", d, ("gr", h))
@@ -507,7 +600,7 @@
 
     def forward(it, h):
         yield need("sp", ("az", it, h), *[("by", it, h, d) for d in range(NZ)])
-        yield from wait_recv(it, ("by", h), NZ * 3 * 24 * 4 * LANES)
+        yield from wait_recv(it, ("by", h), (NZ * 3 - 2 * len(BY_RELAY)) * 24 * 4 * LANES)
         flush(("gx", h), ("sr", h))
 
         def parts(i, carry):
@@ -593,14 +686,19 @@
 
     plan.add(observe(), 0)
     for it in range(ITERS):
-        plan.add(norm(0, it, "xyz"), 0)
-        plan.add(norm(1, it, "yzx"), 0)
+        plan.add(norm(0, it, "wz"), 0)
+        plan.add(norm(1, it, "zw"), 0)
         for h in range(HALVES):
             plan.add(gather_x(it, h), 1 + h)
             plan.add(za(it, h), 1 + h)
             plan.add(zb_end(it, h), 1 + h)
             plan.add(bz(it, h), 1 + h)
             plan.add(az(it, h), 1 + h)
+            for g in range(2):
+                if h in ZA_RELAY:
+                    plan.add(zr(it, h, g), 1 + h)
+                if h in AZ_RELAY:
+                    plan.add(ar(it, h, g), 1 + h)
             for way in WAYS:
                 plan.add(zb(it, h, way), 1 + h)
             for d in ORDER:
@@ -609,7 +707,7 @@
                 plan.add(by(it, h, d), 1 + h)
             plan.add(right(it, h), 1 + h)
             plan.add(forward(it, h), 1 + h)
-    plan.add(norm(0, ITERS, "xyz"), 0)
+    plan.add(norm(0, ITERS, "wz"), 0)
     for h in range(HALVES):
         plan.add(output(0, h, left_out), 3)
         plan.add(output(1, h, sol_out), 2)
@@ -622,10 +720,16 @@
 TOTAL = []
 
 
+def hand_over(sol_in, left_in, sol_out, left_out):
+    sol_out[...] = sol_in[...]
+    left_out[...] = left_in[...]
+
+
 def on_device(kernel, traces, acq_lists, counts):
     vmem = pltpu.VMEM
     two = HALVES
     scratch = [
+        vmem(traces.shape, F32),
         vmem((2, 2, ROWS_REC, 640), F32),
         vmem((960, COLS), BF16),
         vmem((640, COLS), BF16),
@@ -655,27 +759,33 @@
         vmem((two, 3, 16, LANES), F32),
         vmem((two, 3, BLK, LANES), F32),
         vmem((8192, 128), F32),
-        vmem((2, 3, 8, 128), F32),
-        vmem((2, NX, 8, 128), F32),
-        vmem((2, NY, 8, 128), F32),
-        vmem((2, NZ, 8, 128), F32),
+        vmem((64, 1, 128), F32),
+        vmem((2, 2, 1, 128), F32),
+        vmem((2, NX * NY, 1, 128), F32),
+        vmem((2, NZ, 1, 128), F32),
         vmem((two, BLK, LANES), F32),
         vmem((2, two, 2, 24, LANES), F32),
         vmem((2, two, 24, LANES), F32),
         pltpu.SemaphoreType.DMA((GROUPS,)),
         pltpu.SemaphoreType.DMA((COPIES,)),
-        pltpu.SemaphoreType.DMA((1,)),
+        pltpu.SemaphoreType.DMA((2,)),
     ]
     whole = pl.BlockSpec(memory_space=pltpu.VMEM)
-    return pl.pallas_call(
+    made = pl.pallas_call(
         kernel_body,
         out_shape=(jax.ShapeDtypeStruct((ROWS, 2, FREQS, SOURCES), F32),) * 2,
-        in_specs=[pl.BlockSpec(memory_space=pl.ANY), whole, whole, whole],
+        in_specs=[pl.BlockSpec(memory_space=pl.ANY)] * 2 + [whole, whole],
         out_specs=(whole, whole),
         scratch_shapes=scratch,
         compiler_params=pltpu.CompilerParams(
             collective_id=0, has_side_effects=True, vmem_limit_bytes=60 * 1024 * 1024),
     )(kernel, traces, acq_lists, counts)
+    return pl.pallas_call(
+        hand_over,
+        out_shape=(jax.ShapeDtypeStruct((ROWS, 2, FREQS, SOURCES), F32),) * 2,
+        in_specs=[whole, whole],
+        out_specs=(whole, whole),
+    )(*made)
 
 
 def solution(mesh):

time: 145 us -> 141 us (0.972)
  local copies, waits for them, and re-layouts: 3.05 us -> 0 us
  Pallas kernels: 141 us -> 139 us
    pallas_call x1, Pallas kernels: 141 us -> 138 us  [on_device(): pl.pallas_call(kernel_body, out_shape=(jax.ShapeDtypeStruct((ROWS, 2, FRE...]
    unnamed x2 -> x0, local copies, waits for them, and re-layouts: 3.05 us -> none
    pallas_call x0 -> x1, Pallas kernels: none -> 1.6 us  [on_device(): pl.pallas_call(hand_over, out_shape=(jax.ShapeDtypeStruct((ROWS, 2, FREQS...]
where the time goes in v3:
time: 141 us
  Pallas kernels  139 us (99%)
    pallas_call x1, Pallas kernels, on_device(): pl.pallas_call(kernel_body, out_shape=(jax.ShapeDtypeStruct((ROWS, 2, FRE...  138 us

profile of v3, /device:TPU:1, one launch (start us, length us, event | category | flops | bytes accessed | tf_op | source)
XLA Modules:
  0.0 140.6 jit_solution(6702571601484087124)
XLA Ops:
  1.3 137.8 %shard_map.59 = (f32[20,2,2,256]{3,2,1,0:T(2,128)}, f32[20,2,2,256]{3,2,1,0:T(2,128)}) custom-call(f32[2,2,160,640]{3,2,1,0:T(8,128)} %k_hbm.1, f32[1,28,2,2,256]{4,3,2,1,0:T(2,128)} %traces_hbm.1, s32[1,28]{1,0:T(1,128)} %ids_ref.1, s32[1,1]{1,0:T(1,128)S(6)} %copy.6.counts_ref), custom_call_target="tpu_custom_call" | custom-call | tf_op jit(solution)/shard_map/pallas_call | solution.py:774
  139.0 1.6 %shard_map.60 = (f32[20,2,2,256]{3,2,1,0:T(2,128)}, f32[20,2,2,256]{3,2,1,0:T(2,128)}) custom-call(f32[20,2,2,256]{3,2,1,0:T(2,128)} %get-tuple-element.4.sol_in, f32[20,2,2,256]{3,2,1,0:T(2,128)} %get-tuple-element.5.left_in), custom_call_target="tpu_custom_call" | custom-call | tf_op jit(solution)/shard_map/pallas_call | solution.py:783

commit v4 on v3

--- a/solution.py
+++ b/solution.py
@@ -37,8 +37,8 @@
 
 RATE = 51e3
 RATE_CHIP = 600e3
-DELAY = {("c", 0): 0.9, ("z", 1): 2.5, ("z", 2): 3.1, ("z", 3): 3.7, ("z", 4): 4.3}
-DELAY.update({(a, d): 2.8 + 0.2 * d for a in "xy" for d in (1, 2)})
+DELAY = {("c", 0): 0.9, ("z", 1): 1.9, ("z", 2): 2.5, ("z", 3): 3.1, ("z", 4): 3.7}
+DELAY.update({(a, d): 2.2 + 0.2 * d for a in "xy" for d in (1, 2)})
 WAYS = (1, -1)
 
 
@@ -309,10 +309,12 @@
                 pick[pl.ds(start, 256), :], s3[...], dims, preferred_element_type=F32).astype(BF16)
             return carry
 
-        lax.fori_loop(0, COLS // 256, turned, 0)
-        spend(3.0)
+        for low, high in ((0, 2), (2, 4), (4, 5)):
+            lax.fori_loop(low, high, turned, 0)
+            spend(0.8 * (high - low))
+            plan.mark(("kt3", low))
+            yield need(("kt3", low))
         plan.mark("kt3")
-        yield need(("left", 0, 0))
 
         def straight(i, carry):
             start = pl.multiple_of(i * 256, 256)
@@ -320,9 +322,12 @@
                 s3[0:640, :], pick[pl.ds(start, 256), :], dims, preferred_element_type=F32).astype(BF16)
             return carry
 
-        yield need(("gx", 0, HALVES - 1))
-        lax.fori_loop(0, COLS // 256, straight, 0)
-        spend(2.5)
+        yield need(("p", 0, HALVES - 1))
+        for i in range(COLS // 256):
+            lax.fori_loop(i, i + 1, straight, 0)
+            spend(0.65)
+            plan.mark(("sp", i))
+            yield need(("sp", i))
         plan.mark("sp")
 
     def squares(value):
@@ -386,12 +391,12 @@
                 wst[base + 640:base + 640 + ROWS_REC, cols] = (both[i] - high.astype(F32)).astype(BF16)
 
         def tile(i, carry):
-            start = pl.multiple_of(i * 320, 320)
-            out = jnp.dot(kt3[pl.ds(start, 320), :], wst[...], preferred_element_type=F32)
-            p[h, pl.ds(i * 2, 2)] = out.reshape(2, NY, BLK, LANES)
+            start = pl.multiple_of(i * 640, 640)
+            out = jnp.dot(kt3[pl.ds(start, 640), :], wst[...], preferred_element_type=F32)
+            p[h, pl.ds(i * 4, 4)] = out.reshape(4, NY, BLK, LANES)
             return carry
 
-        lax.fori_loop(0, 4, tile, 0)
+        lax.fori_loop(0, 2, tile, 0)
         spend(1.2)
         plan.mark(("p", it, h))
 

time: 141 us -> 140 us (level)
  no operation moved by 1% of the time
where the time goes in v4:
time: 140 us
  Pallas kernels  139 us (99%)
    pallas_call x1, Pallas kernels, on_device(): pl.pallas_call(kernel_body, out_shape=(jax.ShapeDtypeStruct((ROWS, 2, FRE...  137 us

profile of v4, /device:TPU:1, one launch (start us, length us, event | category | flops | bytes accessed | tf_op | source)
XLA Modules:
  0.0 140.2 jit_solution(14561515611317500680)
XLA Ops:
  1.3 137.3 %shard_map.59 = (f32[20,2,2,256]{3,2,1,0:T(2,128)}, f32[20,2,2,256]{3,2,1,0:T(2,128)}) custom-call(f32[2,2,160,640]{3,2,1,0:T(8,128)} %k_hbm.1, f32[1,28,2,2,256]{4,3,2,1,0:T(2,128)} %traces_hbm.1, s32[1,28]{1,0:T(1,128)} %ids_ref.1, s32[1,1]{1,0:T(1,128)S(6)} %copy.6.counts_ref), custom_call_target="tpu_custom_call" | custom-call | tf_op jit(solution)/shard_map/pallas_call | solution.py:779
  138.6 1.6 %shard_map.60 = (f32[20,2,2,256]{3,2,1,0:T(2,128)}, f32[20,2,2,256]{3,2,1,0:T(2,128)}) custom-call(f32[20,2,2,256]{3,2,1,0:T(2,128)} %get-tuple-element.4.sol_in, f32[20,2,2,256]{3,2,1,0:T(2,128)} %get-tuple-element.5.left_in), custom_call_target="tpu_custom_call" | custom-call | tf_op jit(solution)/shard_map/pallas_call | solution.py:788

commit v5 on v4

--- a/solution.py
+++ b/solution.py
@@ -618,12 +618,7 @@
 
         lax.fori_loop(0, NZ, parts, 0)
 
-        def tile(i, carry):
-            rows = pl.ds(pl.multiple_of(i * 320, 320), 320)
-            acc[rows, :] = jnp.dot(sp[rows, :], vh[...], preferred_element_type=F32)
-            return carry
-
-        lax.fori_loop(0, 2, tile, 0)
+        acc[...] = jnp.dot(sp[...], vh[...], preferred_element_type=F32)
         both = acc[0:320, :] + acc[320:640, :] + jnp.dot(sp[0:320, :], vl[...], preferred_element_type=F32)
         real = both[:ROWS_REC, :WIDE] - both[ROWS_REC:, WIDE:]
         imag = both[:ROWS_REC, WIDE:] + both[ROWS_REC:, :WIDE]

time: 140 us -> 141 us (level)
  no operation moved by 1% of the time
where the time goes in v5:
time: 141 us
  Pallas kernels  139 us (99%)
    pallas_call x1, Pallas kernels, on_device(): pl.pallas_call(kernel_body, out_shape=(jax.ShapeDtypeStruct((ROWS, 2, FRE...  138 us

profile of v5, /device:TPU:1, one launch (start us, length us, event | category | flops | bytes accessed | tf_op | source)
XLA Modules:
  0.0 140.7 jit_solution(9767481453348653760)
XLA Ops:
  1.3 137.8 %shard_map.59 = (f32[20,2,2,256]{3,2,1,0:T(2,128)}, f32[20,2,2,256]{3,2,1,0:T(2,128)}) custom-call(f32[2,2,160,640]{3,2,1,0:T(8,128)} %k_hbm.1, f32[1,28,2,2,256]{4,3,2,1,0:T(2,128)} %traces_hbm.1, s32[1,28]{1,0:T(1,128)} %ids_ref.1, s32[1,1]{1,0:T(1,128)S(6)} %copy.6.counts_ref), custom_call_target="tpu_custom_call" | custom-call | tf_op jit(solution)/shard_map/pallas_call | solution.py:774
  139.1 1.6 %shard_map.60 = (f32[20,2,2,256]{3,2,1,0:T(2,128)}, f32[20,2,2,256]{3,2,1,0:T(2,128)}) custom-call(f32[20,2,2,256]{3,2,1,0:T(2,128)} %get-tuple-element.4.sol_in, f32[20,2,2,256]{3,2,1,0:T(2,128)} %get-tuple-element.5.left_in), custom_call_target="tpu_custom_call" | custom-call | tf_op jit(solution)/shard_map/pallas_call | solution.py:783
